TPU v7x, 512 devices: a whole 4x4x16 slice. The times are simulated.
512 devices in a mesh: expert: 128 (over y, x_lo, z), half: 4 (over x_hi, core).
Axes of the slice: x: 4 (x_hi: 2, x_lo: 2; x = x_hi * 2 + x_lo), y: 4, z: 16, core: 2. Of those that a mesh axis runs over, the one named last changes fastest.
Arguments:
- tokens: bfloat16 [25088, 1024], P('expert', 'half'), may hold values from -128 to 128
- slot_params: bfloat16 [1024, 256], P('half'), may hold values from -0.5 to 0.5
- w_up: bfloat16 [128, 1024, 4096], P('expert', None, 'half'), may hold values from -0.1875 to 0.1875
- w_down: bfloat16 [128, 4096, 1024], P('expert', 'half'), may hold values from -0.09375 to 0.09375
- cotangent: bfloat16 [25088, 1024], P('expert', 'half'), may hold values from -6 to 6
Outputs:
- mixed: bfloat16 [25088, 1024], P('expert', 'half')
- grad_tokens: bfloat16 [25088, 1024], P('expert', 'half')
- grad_params: float32 [1024, 256], P('half')
All inputs are finite; a program needn't handle non-finite values.
Results may differ from a plain program's by a relative error of at most 0.017.
Values may be sent and summed in bfloat16 or wider, within the bound.
A program may use at most 64 MiB of HBM per device.

v0:
```python
import jax
import jax.numpy as jnp
from jax import lax
from jax.sharding import PartitionSpec as P

SEQ = 196
SLOTS = 2


def gelu_grad(preact, upstream):
    pullback = jax.vjp(jax.nn.gelu, preact)[1]
    return pullback(upstream)[0]


def softmax_back(probabilities, upstream, over_axis):
    inner = jnp.sum(probabilities * upstream, axis=over_axis, keepdims=True)
    return probabilities * (upstream - inner)


def local(tokens, slot_params, w_up, w_down, cotangent):
    feat_quarter = tokens.shape[1]
    images = tokens.shape[0] // SEQ
    columns = slot_params.shape[1]
    experts = columns // SLOTS
    up_matrix = w_up[0]
    down_matrix = w_down[0]
    inputs = tokens.reshape(images, SEQ, feat_quarter)
    upstream = cotangent.reshape(images, SEQ, feat_quarter)
    partial_logits = jnp.einsum(
        "imf,fc->imc", inputs, slot_params, preferred_element_type=jnp.float32
    )
    logits = lax.psum(partial_logits, "half")
    dispatch = jax.nn.softmax(logits, axis=1)
    combine = jax.nn.softmax(logits, axis=2)
    dispatch_bf = dispatch.astype(jnp.bfloat16).reshape(images, SEQ, experts, SLOTS)
    combine_bf = combine.astype(jnp.bfloat16).reshape(images, SEQ, experts, SLOTS)
    slot_in = jnp.einsum(
        "imes,imf->sife", dispatch_bf, inputs, preferred_element_type=jnp.float32
    ).astype(jnp.bfloat16)
    received = lax.all_to_all(slot_in, "expert", split_axis=3, concat_axis=3, tiled=True)
    up_slice = up_matrix
    preact = jnp.einsum(
        "sifr,fk->sirk",
        lax.all_gather(received, "half", axis=2, tiled=True),
        up_slice,
        preferred_element_type=jnp.float32,
    )
    hidden = jax.nn.gelu(preact).astype(jnp.bfloat16)
    down_slice = down_matrix
    summed = lax.psum(
        jnp.einsum("kf,sirk->fsir", down_slice, hidden, preferred_element_type=jnp.float32).astype(
            jnp.bfloat16
        ),
        "half",
    ).astype(jnp.float32)
    slot_out = lax.dynamic_slice_in_dim(
        summed, lax.axis_index("half") * feat_quarter, feat_quarter, 0
    )
    returned = lax.all_to_all(
        slot_out.astype(jnp.bfloat16), "expert", split_axis=3, concat_axis=3, tiled=True
    )
    mixed = jnp.einsum(
        "imes,fsie->imf", combine_bf, returned, preferred_element_type=jnp.float32
    ).astype(jnp.bfloat16)
    grad_slot_out = jnp.einsum(
        "imes,imf->sife", combine_bf, upstream, preferred_element_type=jnp.float32
    ).astype(jnp.bfloat16)
    combine_part = jnp.einsum(
        "imf,fsie->imes", upstream, returned, preferred_element_type=jnp.float32
    ).reshape(images, SEQ, columns)
    grad_combine = lax.psum(combine_part.astype(jnp.bfloat16), "half").astype(jnp.float32)
    grad_received = lax.all_to_all(grad_slot_out, "expert", split_axis=3, concat_axis=3, tiled=True)
    down_slice = down_matrix
    grad_hidden = jnp.einsum(
        "sifr,kf->sirk",
        lax.all_gather(grad_received, "half", axis=2, tiled=True),
        down_slice,
        preferred_element_type=jnp.float32,
    )
    grad_preact = gelu_grad(preact, grad_hidden).astype(jnp.bfloat16)
    up_slice = up_matrix
    summed_grad = lax.psum(
        jnp.einsum(
            "fk,sirk->fsir", up_slice, grad_preact, preferred_element_type=jnp.float32
        ).astype(jnp.bfloat16),
        "half",
    ).astype(jnp.float32)
    grad_slot_in = lax.dynamic_slice_in_dim(
        summed_grad, lax.axis_index("half") * feat_quarter, feat_quarter, 0
    )
    grad_returned = lax.all_to_all(
        grad_slot_in.astype(jnp.bfloat16), "expert", split_axis=3, concat_axis=3, tiled=True
    )
    dispatch_part = jnp.einsum(
        "imf,fsie->imes", inputs, grad_returned, preferred_element_type=jnp.float32
    ).reshape(images, SEQ, columns)
    grad_dispatch = lax.psum(dispatch_part.astype(jnp.bfloat16), "half").astype(jnp.float32)
    grad_logits = softmax_back(combine, grad_combine, 2) + softmax_back(dispatch, grad_dispatch, 1)
    grad_logit_bf = grad_logits.astype(jnp.bfloat16)
    token_term = jnp.einsum(
        "imes,fsie->imf", dispatch_bf, grad_returned, preferred_element_type=jnp.float32
    )
    logit_term = jnp.einsum(
        "imc,fc->imf", grad_logit_bf, slot_params, preferred_element_type=jnp.float32
    )
    grad_tokens = (token_term + logit_term).astype(jnp.bfloat16).reshape(images * SEQ, feat_quarter)
    params_part = jnp.einsum(
        "imf,imc->fc", inputs, grad_logit_bf, preferred_element_type=jnp.float32
    )
    grad_params = lax.psum(params_part, "expert")
    return (mixed.reshape(images * SEQ, feat_quarter), grad_tokens, grad_params)


def solution(mesh):
    in_specs = (
        P("expert", "half"),
        P("half", None),
        P("expert", None, "half"),
        P("expert", "half", None),
        P("expert", "half"),
    )
    out_specs = (P("expert", "half"), P("expert", "half"), P("half", None))
    return jax.shard_map(local, mesh=mesh, in_specs=in_specs, out_specs=out_specs, check_vma=False)
```

profile of v0, /device:TPU:4, one launch (start us, length us, event | category | flops | bytes accessed | tf_op | source)
XLA Modules:
  0.0 1391.0 jit_solution(2654474292173289853)
XLA Ops:
  7.2 2.0 convolution_bitcast_fusion.3
  9.2 59.9 %all-reduce.7.cloned.1.call-done = f32[1,196,256]{2,1,0:T(8,128)} async-done(((f32[1,196,256]{2,1,0:T(8,128)}), f32[1,196,256]{2,1,0:T(8,128)}) %all-reduce.7.cloned.1.call-update) | async-done | bytes 200720 | tf_op jit(solution)/shard_map/psum | solution.py:32
  69.2 1.0 fusion.82
  70.2 1.1 fusion.60
  71.4 1.1 fusion.80
  72.6 0.1 copy.36
  72.8 0.2 fusion.22
  73.0 0.8 copy.37
  73.8 18.0 %all-to-all-start = ((bf16[2,1,256,128]{2,0,1,3:T(2,128)(2,1)}), bf16[2,1,256,128]{2,0,1,3:T(2,128)(2,1)S(1)}, u32[]{:S(2)}, u32[]{:S(2)}) async-start(bf16[2,1,256,128]{2,0,1,3:T(2,128)(2,1)} %copy.37), calls=%async_computation | async-start | bytes 262144 | tf_op jit(solution)/shard_map/all_to_all | solution.py:40
  92.0 0.1 copy.41
  92.1 0.2 fusion.23
  92.4 0.8 copy.43
  93.2 18.0 %all-to-all-done = bf16[2,1,256,128]{2,0,1,3:T(2,128)(2,1)S(1)} async-done(((bf16[2,1,256,128]{2,0,1,3:T(2,128)(2,1)}), bf16[2,1,256,128]{2,0,1,3:T(2,128)(2,1)S(1)}, u32[]{:S(2)}, u32[]{:S(2)}) %all-to-all-start) | async-done | bytes 131104 | tf_op jit(solution)/shard_map/all_to_all | solution.py:40
  111.2 6.1 all-to-all-start.2
  117.3 8.2 all_gather.6
  125.6 9.4 all-to-all-done.2
  135.0 8.0 all_gather.7
  143.0 2.3 fusion.6
  145.4 1.0 copy-done.3
  146.3 1.6 fusion.14
  148.0 4.5 fusion.17
  152.5 51.2 %all-reduce.13.cloned.1.call-done = (bf16[1024,2,1,128]{0,3,1,2:T(8,128)(2,1)}, bf16[1024,2,1,128]{0,3,1,2:T(8,128)(2,1)}) async-done(((bf16[1024,2,1,128]{0,3,1,2:T(8,128)(2,1)}, bf16[1024,2,1,128]{0,3,1,2:T(8,128)(2,1)}), (bf16[1024,2,1,128]{0,3,1,2:T(8,128)(2,1)}, bf16[1024,2,1,128]{0,3,1,2:T(8,128)(2,1)})) %all-reduce.13.cloned.1.call-update) | async-done | bytes 1048592 | tf_op jit(solution)/shard_map/psum | solution.py:50
  203.7 0.9 convert_convert_fusion
  204.6 0.8 copy.45
  205.4 18.0 %all-to-all-start.3 = ((bf16[256,2,1,128]{0,1,2,3:T(2,128)(2,1)}), bf16[256,2,1,128]{0,1,2,3:T(2,128)(2,1)S(1)}, u32[]{:S(2)}, u32[]{:S(2)}) async-start(bf16[256,2,1,128]{0,1,2,3:T(2,128)(2,1)} %copy.45), calls=%async_computation.3 | async-start | bytes 262144 | tf_op jit(solution)/shard_map/all_to_all | solution.py:91
  223.5 0.9 convert_convert_fusion.1
  224.4 0.8 copy.39
  225.2 16.9 %all-to-all-done.3 = bf16[256,2,1,128]{0,1,2,3:T(2,128)(2,1)S(1)} async-done(((bf16[256,2,1,128]{0,1,2,3:T(2,128)(2,1)}), bf16[256,2,1,128]{0,1,2,3:T(2,128)(2,1)S(1)}, u32[]{:S(2)}, u32[]{:S(2)}) %all-to-all-start.3) | async-done | bytes 131104 | tf_op jit(solution)/shard_map/all_to_all | solution.py:91
  242.1 6.4 all-to-all-start.1
  248.5 0.1 copy.46
  248.6 0.2 fusion.25
  248.8 0.2 copy.50
  249.0 0.1 convert_element_type.156
  249.2 0.7 copy.51
  249.9 15.6 %all-to-all-done.1 = bf16[256,2,1,128]{0,1,2,3:T(2,128)(2,1)S(1)} async-done(((bf16[256,2,1,128]{0,1,2,3:T(2,128)(2,1)}), bf16[256,2,1,128]{0,1,2,3:T(2,128)(2,1)S(1)}, u32[]{:S(2)}, u32[]{:S(2)}) %all-to-all-start.1) | async-done | bytes 131104 | tf_op jit(solution)/shard_map/all_to_all | solution.py:59
  265.5 0.1 copy.40
  265.7 0.2 fusion.24
  265.8 0.2 copy.48
  266.2 0.7 copy.49
  267.0 0.9 fusion.20
  267.8 42.0 %all-reduce.11.cloned.1.call-done = (bf16[1,196,256]{2,1,0:T(8,128)(2,1)}, bf16[1,196,256]{2,1,0:T(8,128)(2,1)}) async-done(((bf16[1,196,256]{2,1,0:T(8,128)(2,1)}, bf16[1,196,256]{2,1,0:T(8,128)(2,1)}), (bf16[1,196,256]{2,1,0:T(8,128)(2,1)}, bf16[1,196,256]{2,1,0:T(8,128)(2,1)})) %all-reduce.11.cloned.1.call-update) | async-done | bytes 200720 | tf_op jit(solution)/shard_map/psum | solution.py:97
  309.9 1.2 fusion.51
  311.1 1.1 fusion.65
  312.2 0.9 convolution_bitcast_fusion
  313.1 0.2 convolution_bitcast_fusion.1
  313.4 0.9 fusion.21
  314.2 1068.4 %all-reduce.9.cloned.1.call-done = f32[256,256]{0,1:T(8,128)} async-done(((f32[256,256]{0,1:T(8,128)}), f32[256,256]{0,1:T(8,128)}) %all-reduce.9.cloned.1.call-update) | async-done | bytes 262160 | tf_op jit(solution)/shard_map/psum | solution.py:110
  1382.7 1.8 copy.52
  (42 shorter events, 0.8 us)
Async XLA Ops:
  7.2 139.2 %copy-start = (bf16[1,1024,1024]{2,1,0:T(8,128)(2,1)S(1)}, bf16[1,1024,1024]{2,1,0:T(8,128)(2,1)}, u32[]{:S(2)}) copy-start(bf16[1,1024,1024]{2,1,0:T(8,128)(2,1)} %param.8) | copy-start | bytes 6291460
  7.2 65.6 %copy-start.2 = (bf16[196,256]{1,0:T(8,128)(2,1)S(1)}, bf16[196,256]{1,0:T(8,128)(2,1)}, u32[]{:S(2)}) copy-start(bf16[196,256]{1,0:T(8,128)(2,1)} %param.5) | copy-start | bytes 301060
  7.2 84.9 %copy-start.5 = (bf16[196,256]{1,0:T(8,128)(2,1)S(1)}, bf16[196,256]{1,0:T(8,128)(2,1)}, u32[]{:S(2)}) copy-start(bf16[196,256]{1,0:T(8,128)(2,1)} %param.9) | copy-start | bytes 301060
  7.2 62.0 %all-reduce.7.cloned.1.call-start = ((), (), s32[]{:S(2)}) async-start(), calls=%async_computation.4 | async-start | bytes 409600 | tf_op jit(solution)/shard_map/psum | solution.py:32
  70.2 2.2 copy-start.6
  70.2 2.2 copy-start.8
  71.3 1.1 copy-start.10
  71.3 1.1 copy-start.12
  73.8 37.3 %all-to-all-start = ((bf16[2,1,256,128]{2,0,1,3:T(2,128)(2,1)}), bf16[2,1,256,128]{2,0,1,3:T(2,128)(2,1)S(1)}, u32[]{:S(2)}, u32[]{:S(2)}) async-start(bf16[2,1,256,128]{2,0,1,3:T(2,128)(2,1)} %copy.37), calls=%async_computation | async-start | bytes 262144 | tf_op jit(solution)/shard_map/all_to_all | solution.py:40
  111.2 23.8 %all-to-all-start.2 = ((bf16[2,1,256,128]{2,0,1,3:T(2,128)(2,1)}), bf16[2,1,256,128]{2,0,1,3:T(2,128)(2,1)S(1)}, u32[]{:S(2)}, u32[]{:S(2)}) async-start(bf16[2,1,256,128]{2,0,1,3:T(2,128)(2,1)} %copy.43), calls=%async_computation.2 | async-start | bytes 262144 | tf_op jit(solution)/shard_map/all_to_all | solution.py:72
  117.3 86.4 %all-reduce.13.cloned.1.call-start = ((), (), s32[]{:S(2)}) async-start(), calls=%async_computation.7 | async-start | bytes 2097152 | tf_op jit(solution)/shard_map/psum | solution.py:50
  145.3 1.0 copy-start.3
  205.4 104.5 %copy-start.1 = (f32[1,196,256]{2,1,0:T(8,128)S(1)}, f32[1,196,256]{2,1,0:T(8,128)}, u32[]{:S(2)}) copy-start(f32[1,196,256]{2,1,0:T(8,128)} %all-reduce.7.cloned.1.call-done) | copy-start | bytes 602116
  205.4 104.5 %copy-start.7 = (f32[256]{0:T(256)S(1)}, f32[256]{0:T(256)}, u32[]{:S(2)}) copy-start(f32[256]{0:T(256)} %copy-done.6) | copy-start | bytes 3076
  205.4 104.5 %copy-start.9 = (f32[196]{0:T(256)S(1)}, f32[196]{0:T(256)}, u32[]{:S(2)}) copy-start(f32[196]{0:T(256)} %copy-done.8) | copy-start | bytes 2356
  205.4 104.5 %copy-start.11 = (f32[256]{0:T(256)S(1)}, f32[256]{0:T(256)}, u32[]{:S(2)}) copy-start(f32[256]{0:T(256)} %copy-done.10) | copy-start | bytes 3076
  205.4 104.5 %copy-start.13 = (f32[196]{0:T(256)S(1)}, f32[196]{0:T(256)}, u32[]{:S(2)}) copy-start(f32[196]{0:T(256)} %copy-done.12) | copy-start | bytes 2356
  205.4 36.7 %all-to-all-start.3 = ((bf16[256,2,1,128]{0,1,2,3:T(2,128)(2,1)}), bf16[256,2,1,128]{0,1,2,3:T(2,128)(2,1)S(1)}, u32[]{:S(2)}, u32[]{:S(2)}) async-start(bf16[256,2,1,128]{0,1,2,3:T(2,128)(2,1)} %copy.45), calls=%async_computation.3 | async-start | bytes 262144 | tf_op jit(solution)/shard_map/all_to_all | solution.py:91
  242.1 23.4 %all-to-all-start.1 = ((bf16[256,2,1,128]{0,1,2,3:T(2,128)(2,1)}), bf16[256,2,1,128]{0,1,2,3:T(2,128)(2,1)S(1)}, u32[]{:S(2)}, u32[]{:S(2)}) async-start(bf16[256,2,1,128]{0,1,2,3:T(2,128)(2,1)} %copy.39), calls=%async_computation.1 | async-start | bytes 262144 | tf_op jit(solution)/shard_map/all_to_all | solution.py:59
  248.4 61.4 %all-reduce.11.cloned.1.call-start = ((), (), s32[]{:S(2)}) async-start(), calls=%async_computation.6 | async-start | bytes 409600 | tf_op jit(solution)/shard_map/psum | solution.py:97
  249.1 64.2 %copy-start.4 = (bf16[256,256]{1,0:T(8,128)(2,1)S(1)}, bf16[256,256]{1,0:T(8,128)(2,1)}, u32[]{:S(2)}) copy-start(bf16[256,256]{1,0:T(8,128)(2,1)} %param.6) | copy-start | bytes 393220
  266.9 1115.7 %all-reduce.9.cloned.1.call-start = ((), (), s32[]{:S(2)}) async-start(), calls=%async_computation.5 | async-start | bytes 524288 | tf_op jit(solution)/shard_map/psum | solution.py:110
Sparse Core Ops, SparseCore 0:
  11.5 57.5 all-reduce.6
  152.6 51.0 all-reduce.12
  267.0 42.7 all-reduce.10
  313.3 1069.3 all-reduce.8
where the time goes:
time: 1390 us
  waiting for transfers between devices  1280 us (92%)
  starting transfers between devices  48.6 us (3%)
  blocking collectives  16.2 us (1%)
  matrix products  14.2 us (1%)
  between operations  14.1 us (1%)
    psum x1, waiting for transfers between devices, local(): grad_params = lax.psum(params_part, 'expert')  1070 us
    psum x1, waiting for transfers between devices, local(): logits = lax.psum(partial_logits, 'half')  59.9 us
    psum x1, waiting for transfers between devices, local(): lax.psum(jnp.einsum('kf,sirk->fsir', down_slice, hidden, preferred_elemen...  51.2 us
    psum x1, waiting for transfers between devices, local(): lax.psum(dispatch_part.astype(jnp.bfloat16), 'half').astype(jnp.float32)  42 us
  transfers between devices with their start and end apart: 8, of which 8 were waited for; matrix products, arithmetic and copies ran while one was open for 0% of the time, Pallas kernels for 0%

commit v1 on v0

--- a/solution.py
+++ b/solution.py
@@ -5,6 +5,8 @@
 
 SEQ = 196
 SLOTS = 2
+EXPERT = ("y", "x_lo", "z")
+HALF = ("x_hi", "core")
 
 
 def gelu_grad(preact, upstream):
@@ -29,7 +31,7 @@
     partial_logits = jnp.einsum(
         "imf,fc->imc", inputs, slot_params, preferred_element_type=jnp.float32
     )
-    logits = lax.psum(partial_logits, "half")
+    logits = lax.psum(partial_logits, HALF)
     dispatch = jax.nn.softmax(logits, axis=1)
     combine = jax.nn.softmax(logits, axis=2)
     dispatch_bf = dispatch.astype(jnp.bfloat16).reshape(images, SEQ, experts, SLOTS)
@@ -37,11 +39,11 @@
     slot_in = jnp.einsum(
         "imes,imf->sife", dispatch_bf, inputs, preferred_element_type=jnp.float32
     ).astype(jnp.bfloat16)
-    received = lax.all_to_all(slot_in, "expert", split_axis=3, concat_axis=3, tiled=True)
+    received = lax.all_to_all(slot_in, EXPERT, split_axis=3, concat_axis=3, tiled=True)
     up_slice = up_matrix
     preact = jnp.einsum(
         "sifr,fk->sirk",
-        lax.all_gather(received, "half", axis=2, tiled=True),
+        lax.all_gather(received, HALF, axis=2, tiled=True),
         up_slice,
         preferred_element_type=jnp.float32,
     )
@@ -51,13 +53,13 @@
         jnp.einsum("kf,sirk->fsir", down_slice, hidden, preferred_element_type=jnp.float32).astype(
             jnp.bfloat16
         ),
-        "half",
+        HALF,
     ).astype(jnp.float32)
     slot_out = lax.dynamic_slice_in_dim(
-        summed, lax.axis_index("half") * feat_quarter, feat_quarter, 0
+        summed, lax.axis_index(HALF) * feat_quarter, feat_quarter, 0
     )
     returned = lax.all_to_all(
-        slot_out.astype(jnp.bfloat16), "expert", split_axis=3, concat_axis=3, tiled=True
+        slot_out.astype(jnp.bfloat16), EXPERT, split_axis=3, concat_axis=3, tiled=True
     )
     mixed = jnp.einsum(
         "imes,fsie->imf", combine_bf, returned, preferred_element_type=jnp.float32
@@ -68,12 +70,12 @@
     combine_part = jnp.einsum(
         "imf,fsie->imes", upstream, returned, preferred_element_type=jnp.float32
     ).reshape(images, SEQ, columns)
-    grad_combine = lax.psum(combine_part.astype(jnp.bfloat16), "half").astype(jnp.float32)
-    grad_received = lax.all_to_all(grad_slot_out, "expert", split_axis=3, concat_axis=3, tiled=True)
+    grad_combine = lax.psum(combine_part.astype(jnp.bfloat16), HALF).astype(jnp.float32)
+    grad_received = lax.all_to_all(grad_slot_out, EXPERT, split_axis=3, concat_axis=3, tiled=True)
     down_slice = down_matrix
     grad_hidden = jnp.einsum(
         "sifr,kf->sirk",
-        lax.all_gather(grad_received, "half", axis=2, tiled=True),
+        lax.all_gather(grad_received, HALF, axis=2, tiled=True),
         down_slice,
         preferred_element_type=jnp.float32,
     )
@@ -83,18 +85,18 @@
         jnp.einsum(
             "fk,sirk->fsir", up_slice, grad_preact, preferred_element_type=jnp.float32
         ).astype(jnp.bfloat16),
-        "half",
+        HALF,
     ).astype(jnp.float32)
     grad_slot_in = lax.dynamic_slice_in_dim(
-        summed_grad, lax.axis_index("half") * feat_quarter, feat_quarter, 0
+        summed_grad, lax.axis_index(HALF) * feat_quarter, feat_quarter, 0
     )
     grad_returned = lax.all_to_all(
-        grad_slot_in.astype(jnp.bfloat16), "expert", split_axis=3, concat_axis=3, tiled=True
+        grad_slot_in.astype(jnp.bfloat16), EXPERT, split_axis=3, concat_axis=3, tiled=True
     )
     dispatch_part = jnp.einsum(
         "imf,fsie->imes", inputs, grad_returned, preferred_element_type=jnp.float32
     ).reshape(images, SEQ, columns)
-    grad_dispatch = lax.psum(dispatch_part.astype(jnp.bfloat16), "half").astype(jnp.float32)
+    grad_dispatch = lax.psum(dispatch_part.astype(jnp.bfloat16), HALF).astype(jnp.float32)
     grad_logits = softmax_back(combine, grad_combine, 2) + softmax_back(dispatch, grad_dispatch, 1)
     grad_logit_bf = grad_logits.astype(jnp.bfloat16)
     token_term = jnp.einsum(
@@ -107,17 +109,18 @@
     params_part = jnp.einsum(
         "imf,imc->fc", inputs, grad_logit_bf, preferred_element_type=jnp.float32
     )
-    grad_params = lax.psum(params_part, "expert")
+    grad_params = lax.psum(lax.psum(lax.psum(params_part, "z"), "y"), "x_lo")
     return (mixed.reshape(images * SEQ, feat_quarter), grad_tokens, grad_params)
 
 
 def solution(mesh):
+    mesh = jax.sharding.Mesh(mesh.devices.reshape(4, 2, 16, 2, 2), EXPERT + HALF)
     in_specs = (
-        P("expert", "half"),
-        P("half", None),
-        P("expert", None, "half"),
-        P("expert", "half", None),
-        P("expert", "half"),
+        P(EXPERT, HALF),
+        P(HALF, None),
+        P(EXPERT, None, HALF),
+        P(EXPERT, HALF, None),
+        P(EXPERT, HALF),
     )
-    out_specs = (P("expert", "half"), P("expert", "half"), P("half", None))
+    out_specs = (P(EXPERT, HALF), P(EXPERT, HALF), P(HALF, None))
     return jax.shard_map(local, mesh=mesh, in_specs=in_specs, out_specs=out_specs, check_vma=False)

time: 1390 us -> 567 us (0.41)
  the two profiles are of different devices: /device:TPU:4 before, /device:TPU:1 now
where the time goes in v1:
time: 567 us; the launch traced here: 566 us
  waiting for transfers between devices  453 us (80%)
  starting transfers between devices  46.9 us (8%)
  blocking collectives  21.4 us (4%)
  between operations  14.5 us (3%)
  matrix products  14.1 us (2%)
  local copies, waits for them, and re-layouts  8.99 us (2%)
  other arithmetic  7.34 us (1%)
    psum x3, waiting for transfers between devices, local(): grad_params = lax.psum(lax.psum(lax.psum(params_part, 'z'), 'y'), 'x_lo')  238 us
    psum x1, waiting for transfers between devices, local(): logits = lax.psum(partial_logits, HALF)  64.2 us
    psum x1, waiting for transfers between devices, local(): lax.psum(jnp.einsum('kf,sirk->fsir', down_slice, hidden, preferred_elemen...  52.4 us
    psum x1, waiting for transfers between devices, local(): lax.psum(dispatch_part.astype(jnp.bfloat16), HALF).astype(jnp.float32)  48.2 us
    all_to_all x1, starting transfers between devices, local(): lax.all_to_all(grad_slot_in.astype(jnp.bfloat16), EXPERT, split_axis=3, c...  16.6 us
    all_to_all x1, starting transfers between devices, local(): lax.all_to_all(slot_in, EXPERT, split_axis=3, concat_axis=3, tiled=True)  16.6 us
    all_to_all x1, waiting for transfers between devices, local(): lax.all_to_all(slot_in, EXPERT, split_axis=3, concat_axis=3, tiled=True)  15.3 us
    all_to_all x1, waiting for transfers between devices, local(): lax.all_to_all(grad_slot_in.astype(jnp.bfloat16), EXPERT, split_axis=3, c...  15 us
  transfers between devices with their start and end apart: 10, of which 10 were waited for; matrix products, arithmetic and copies ran while one was open for 1% of the time, Pallas kernels for 0%

profile of v1, /device:TPU:1, one launch (start us, length us, event | category | flops | bytes accessed | tf_op | source)
XLA Modules:
  0.0 566.3 jit_solution(11431547479652277655)
XLA Ops:
  7.2 2.0 convolution_bitcast_fusion.3
  9.2 64.2 %all-reduce.9.cloned.1.call-done = f32[1,196,256]{2,1,0:T(8,128)} async-done(((f32[1,196,256]{2,1,0:T(8,128)}), f32[1,196,256]{2,1,0:T(8,128)}) %all-reduce.9.cloned.1.call-update) | async-done | bytes 200720 | tf_op jit(solution)/shard_map/psum | solution.py:34
  73.4 1.0 fusion.82
  74.5 1.1 fusion.60
  75.6 1.1 fusion.80
  76.9 0.1 copy.36
  77.1 0.2 fusion.22
  77.3 0.8 copy.37
  78.1 16.6 %all-to-all-start = ((bf16[2,1,256,128]{2,0,1,3:T(2,128)(2,1)}), bf16[2,1,256,128]{2,0,1,3:T(2,128)(2,1)S(1)}, u32[]{:S(2)}, u32[]{:S(2)}) async-start(bf16[2,1,256,128]{2,0,1,3:T(2,128)(2,1)} %copy.37), calls=%async_computation | async-start | bytes 262144 | tf_op jit(solution)/shard_map/all_to_all | solution.py:42
  95.1 0.2 fusion.23
  95.3 0.8 copy.43
  96.1 15.3 %all-to-all-done = bf16[2,1,256,128]{2,0,1,3:T(2,128)(2,1)S(1)} async-done(((bf16[2,1,256,128]{2,0,1,3:T(2,128)(2,1)}), bf16[2,1,256,128]{2,0,1,3:T(2,128)(2,1)S(1)}, u32[]{:S(2)}, u32[]{:S(2)}) %all-to-all-start) | async-done | bytes 131104 | tf_op jit(solution)/shard_map/all_to_all | solution.py:42
  111.4 6.6 %all-to-all-start.2 = ((bf16[2,1,256,128]{2,0,1,3:T(2,128)(2,1)}), bf16[2,1,256,128]{2,0,1,3:T(2,128)(2,1)S(1)}, u32[]{:S(2)}, u32[]{:S(2)}) async-start(bf16[2,1,256,128]{2,0,1,3:T(2,128)(2,1)} %copy.43), calls=%async_computation.2 | async-start | bytes 262144 | tf_op jit(solution)/shard_map/all_to_all | solution.py:74
  118.1 10.0 %all_gather.6 = bf16[2,1,1024,128]{2,3,0,1:T(8,128)(2,1)S(1)} all-gather(bf16[2,1,256,128]{2,3,0,1:T(8,128)(2,1)S(1)} %copy.38), channel_id=1, replica_groups=mesh['y'=4,'x_lo'=2,'z'=16,'x_hi'=2,'core'=2] {'x_hi','core'}, dimensions={2}, use_global_device_ids=true | all-gather | bytes 655360 | tf_op jit(solution)/shard_map/all_gather | solution.py:46
  128.1 5.5 all-to-all-done.2
  133.6 11.5 %all_gather.7 = bf16[2,1,1024,128]{2,3,0,1:T(8,128)(2,1)S(1)} all-gather(bf16[2,1,256,128]{2,3,0,1:T(8,128)(2,1)S(1)} %copy.44), channel_id=1, replica_groups=mesh['y'=4,'x_lo'=2,'z'=16,'x_hi'=2,'core'=2] {'x_hi','core'}, dimensions={2}, use_global_device_ids=true | all-gather | bytes 655360 | tf_op jit(solution)/shard_map/all_gather | solution.py:78
  145.1 2.3 fusion.6
  147.4 1.0 copy-done.3
  148.4 1.6 fusion.14
  150.0 4.5 fusion.17
  154.5 52.4 %all-reduce.19.cloned.1.call-done = (bf16[1024,2,1,128]{0,3,1,2:T(8,128)(2,1)}, bf16[1024,2,1,128]{0,3,1,2:T(8,128)(2,1)}) async-done(((bf16[1024,2,1,128]{0,3,1,2:T(8,128)(2,1)}, bf16[1024,2,1,128]{0,3,1,2:T(8,128)(2,1)}), (bf16[1024,2,1,128]{0,3,1,2:T(8,128)(2,1)}, bf16[1024,2,1,128]{0,3,1,2:T(8,128)(2,1)})) %all-reduce.19.cloned.1.call-update) | async-done | bytes 1048592 | tf_op jit(solution)/shard_map/psum | solution.py:52
  207.0 0.9 convert_convert_fusion
  207.9 0.8 copy.45
  208.7 16.6 %all-to-all-start.3 = ((bf16[256,2,1,128]{0,1,2,3:T(2,128)(2,1)}), bf16[256,2,1,128]{0,1,2,3:T(2,128)(2,1)S(1)}, u32[]{:S(2)}, u32[]{:S(2)}) async-start(bf16[256,2,1,128]{0,1,2,3:T(2,128)(2,1)} %copy.45), calls=%async_computation.3 | async-start | bytes 262144 | tf_op jit(solution)/shard_map/all_to_all | solution.py:93
  225.3 0.9 convert_convert_fusion.1
  226.2 0.8 copy.39
  227.0 15.0 %all-to-all-done.3 = bf16[256,2,1,128]{0,1,2,3:T(2,128)(2,1)S(1)} async-done(((bf16[256,2,1,128]{0,1,2,3:T(2,128)(2,1)}), bf16[256,2,1,128]{0,1,2,3:T(2,128)(2,1)S(1)}, u32[]{:S(2)}, u32[]{:S(2)}) %all-to-all-start.3) | async-done | bytes 131104 | tf_op jit(solution)/shard_map/all_to_all | solution.py:93
  242.0 6.8 %all-to-all-start.1 = ((bf16[256,2,1,128]{0,1,2,3:T(2,128)(2,1)}), bf16[256,2,1,128]{0,1,2,3:T(2,128)(2,1)S(1)}, u32[]{:S(2)}, u32[]{:S(2)}) async-start(bf16[256,2,1,128]{0,1,2,3:T(2,128)(2,1)} %copy.39), calls=%async_computation.1 | async-start | bytes 262144 | tf_op jit(solution)/shard_map/all_to_all | solution.py:61
  248.9 0.1 copy.46
  249.0 0.2 fusion.25
  249.2 0.2 copy.50
  249.5 0.7 copy.51
  250.3 14.1 %all-to-all-done.1 = bf16[256,2,1,128]{0,1,2,3:T(2,128)(2,1)S(1)} async-done(((bf16[256,2,1,128]{0,1,2,3:T(2,128)(2,1)}), bf16[256,2,1,128]{0,1,2,3:T(2,128)(2,1)S(1)}, u32[]{:S(2)}, u32[]{:S(2)}) %all-to-all-start.1) | async-done | bytes 131104 | tf_op jit(solution)/shard_map/all_to_all | solution.py:61
  264.3 0.1 copy.40
  264.5 0.2 fusion.24
  264.7 0.2 copy.48
  265.0 0.7 copy.49
  265.8 48.2 %all-reduce.17.cloned.1.call-done = (bf16[1,196,256]{2,1,0:T(8,128)(2,1)}, bf16[1,196,256]{2,1,0:T(8,128)(2,1)}) async-done(((bf16[1,196,256]{2,1,0:T(8,128)(2,1)}, bf16[1,196,256]{2,1,0:T(8,128)(2,1)}), (bf16[1,196,256]{2,1,0:T(8,128)(2,1)}, bf16[1,196,256]{2,1,0:T(8,128)(2,1)})) %all-reduce.17.cloned.1.call-update) | async-done | bytes 200720 | tf_op jit(solution)/shard_map/psum | solution.py:99
  314.0 1.2 fusion.51
  315.2 1.1 fusion.65
  316.3 0.9 convolution_bitcast_fusion
  317.3 126.5 %all-reduce.11.cloned.1.call-done = f32[256,256]{0,1:T(8,128)} async-done(((f32[256,256]{0,1:T(8,128)}), f32[256,256]{0,1:T(8,128)}) %all-reduce.11.cloned.1.call-update) | async-done | bytes 262160 | tf_op jit(solution)/shard_map/psum | solution.py:112
  443.9 0.9 fusion.20
  444.8 62.7 %all-reduce.13.cloned.1.call-done = f32[256,256]{0,1:T(8,128)} async-done(((f32[256,256]{0,1:T(8,128)}), f32[256,256]{0,1:T(8,128)}) %all-reduce.13.cloned.1.call-update) | async-done | bytes 262160 | tf_op jit(solution)/shard_map/psum | solution.py:112
  507.5 0.2 convolution_bitcast_fusion.1
  507.7 0.9 fusion.21
  508.6 49.1 %all-reduce.15.cloned.1.call-done = f32[256,256]{0,1:T(8,128)} async-done(((f32[256,256]{0,1:T(8,128)}), f32[256,256]{0,1:T(8,128)}) %all-reduce.15.cloned.1.call-update) | async-done | bytes 262160 | tf_op jit(solution)/shard_map/psum | solution.py:112
  557.6 1.8 copy.52
  (50 shorter events, 1.2 us)
Async XLA Ops:
  7.2 141.2 %copy-start = (bf16[1,1024,1024]{2,1,0:T(8,128)(2,1)S(1)}, bf16[1,1024,1024]{2,1,0:T(8,128)(2,1)}, u32[]{:S(2)}) copy-start(bf16[1,1024,1024]{2,1,0:T(8,128)(2,1)} %param.8) | copy-start | bytes 6291460
  7.2 69.9 %copy-start.2 = (bf16[196,256]{1,0:T(8,128)(2,1)S(1)}, bf16[196,256]{1,0:T(8,128)(2,1)}, u32[]{:S(2)}) copy-start(bf16[196,256]{1,0:T(8,128)(2,1)} %param.5) | copy-start | bytes 301060
  7.2 87.9 %copy-start.5 = (bf16[196,256]{1,0:T(8,128)(2,1)S(1)}, bf16[196,256]{1,0:T(8,128)(2,1)}, u32[]{:S(2)}) copy-start(bf16[196,256]{1,0:T(8,128)(2,1)} %param.9) | copy-start | bytes 301060
  7.2 66.2 %all-reduce.9.cloned.1.call-start = ((), (), s32[]{:S(2)}) async-start(), calls=%async_computation.4 | async-start | bytes 409600 | tf_op jit(solution)/shard_map/psum | solution.py:34
  74.5 2.2 copy-start.7
  74.5 2.2 copy-start.9
  75.6 1.1 copy-start.11
  75.6 1.1 copy-start.13
  78.1 33.3 %all-to-all-start = ((bf16[2,1,256,128]{2,0,1,3:T(2,128)(2,1)}), bf16[2,1,256,128]{2,0,1,3:T(2,128)(2,1)S(1)}, u32[]{:S(2)}, u32[]{:S(2)}) async-start(bf16[2,1,256,128]{2,0,1,3:T(2,128)(2,1)} %copy.37), calls=%async_computation | async-start | bytes 262144 | tf_op jit(solution)/shard_map/all_to_all | solution.py:42
  111.4 22.2 %all-to-all-start.2 = ((bf16[2,1,256,128]{2,0,1,3:T(2,128)(2,1)}), bf16[2,1,256,128]{2,0,1,3:T(2,128)(2,1)S(1)}, u32[]{:S(2)}, u32[]{:S(2)}) async-start(bf16[2,1,256,128]{2,0,1,3:T(2,128)(2,1)} %copy.43), calls=%async_computation.2 | async-start | bytes 262144 | tf_op jit(solution)/shard_map/all_to_all | solution.py:74
  118.1 88.9 %all-reduce.19.cloned.1.call-start = ((), (), s32[]{:S(2)}) async-start(), calls=%async_computation.9 | async-start | bytes 2097152 | tf_op jit(solution)/shard_map/psum | solution.py:52
  147.4 1.0 copy-start.3
  154.5 110.0 %copy-start.6 = (bf16[196,256]{1,0:T(8,128)(2,1)S(1)}, bf16[196,256]{1,0:T(8,128)(2,1)}, u32[]{:S(2)}) copy-start(bf16[196,256]{1,0:T(8,128)(2,1)} %param.9) | copy-start | bytes 301060
  207.9 106.2 %copy-start.1 = (f32[1,196,256]{2,1,0:T(8,128)S(1)}, f32[1,196,256]{2,1,0:T(8,128)}, u32[]{:S(2)}) copy-start(f32[1,196,256]{2,1,0:T(8,128)} %all-reduce.9.cloned.1.call-done) | copy-start | bytes 602116
  207.9 106.1 %copy-start.8 = (f32[256]{0:T(256)S(1)}, f32[256]{0:T(256)}, u32[]{:S(2)}) copy-start(f32[256]{0:T(256)} %copy-done.7) | copy-start | bytes 3076
  207.9 106.1 %copy-start.10 = (f32[196]{0:T(256)S(1)}, f32[196]{0:T(256)}, u32[]{:S(2)}) copy-start(f32[196]{0:T(256)} %copy-done.9) | copy-start | bytes 2356
  207.9 106.1 %copy-start.12 = (f32[256]{0:T(256)S(1)}, f32[256]{0:T(256)}, u32[]{:S(2)}) copy-start(f32[256]{0:T(256)} %copy-done.11) | copy-start | bytes 3076
  207.9 106.1 %copy-start.14 = (f32[196]{0:T(256)S(1)}, f32[196]{0:T(256)}, u32[]{:S(2)}) copy-start(f32[196]{0:T(256)} %copy-done.13) | copy-start | bytes 2356
  208.7 33.3 %all-to-all-start.3 = ((bf16[256,2,1,128]{0,1,2,3:T(2,128)(2,1)}), bf16[256,2,1,128]{0,1,2,3:T(2,128)(2,1)S(1)}, u32[]{:S(2)}, u32[]{:S(2)}) async-start(bf16[256,2,1,128]{0,1,2,3:T(2,128)(2,1)} %copy.45), calls=%async_computation.3 | async-start | bytes 262144 | tf_op jit(solution)/shard_map/all_to_all | solution.py:93
  242.0 22.3 %all-to-all-start.1 = ((bf16[256,2,1,128]{0,1,2,3:T(2,128)(2,1)}), bf16[256,2,1,128]{0,1,2,3:T(2,128)(2,1)S(1)}, u32[]{:S(2)}, u32[]{:S(2)}) async-start(bf16[256,2,1,128]{0,1,2,3:T(2,128)(2,1)} %copy.39), calls=%async_computation.1 | async-start | bytes 262144 | tf_op jit(solution)/shard_map/all_to_all | solution.py:61
  248.8 65.2 %all-reduce.17.cloned.1.call-start = ((), (), s32[]{:S(2)}) async-start(), calls=%async_computation.8 | async-start | bytes 409600 | tf_op jit(solution)/shard_map/psum | solution.py:99
  264.5 243.2 %copy-start.4 = (bf16[256,256]{1,0:T(8,128)(2,1)S(1)}, bf16[256,256]{1,0:T(8,128)(2,1)}, u32[]{:S(2)}) copy-start(bf16[256,256]{1,0:T(8,128)(2,1)} %param.6) | copy-start | bytes 393220
  265.8 178.0 %all-reduce.11.cloned.1.call-start = ((), (), s32[]{:S(2)}) async-start(), calls=%async_computation.5 | async-start | bytes 524288 | tf_op jit(solution)/shard_map/psum | solution.py:112
  317.3 190.1 %all-reduce.13.cloned.1.call-start = ((), (), s32[]{:S(2)}) async-start(), calls=%async_computation.6 | async-start | bytes 524288 | tf_op jit(solution)/shard_map/psum | solution.py:112
  443.9 113.8 %all-reduce.15.cloned.1.call-start = ((), (), s32[]{:S(2)}) async-start(), calls=%async_computation.7 | async-start | bytes 524288 | tf_op jit(solution)/shard_map/psum | solution.py:112
Sparse Core Ops, SparseCore 0:
  11.5 61.8 all-reduce.8
  154.7 52.2 all-reduce.18
  265.9 48.0 all-reduce.16
  317.4 126.3 all-reduce.10
  446.0 61.3 all-reduce.12
  510.2 47.4 all-reduce.14

commit v2 on v1

v2 whole, which is shorter than its diff:
```python
import functools

import jax
import jax.numpy as jnp
from jax import lax
from jax.experimental import pallas as pl
from jax.experimental.pallas import tpu as pltpu
from jax.sharding import PartitionSpec as P

SEQ = 196
BF16 = jnp.bfloat16
F32 = jnp.float32
EXPERT = ("y", "x_lo", "z")
HALF = ("x_hi", "core")
MESH = pl.DeviceIdType.MESH
GELU_C = 0.7978845608
GELU_A = 0.044715


def dot(a, b, ca, cb):
    return lax.dot_general(a, b, (((ca,), (cb,)), ((), ())), preferred_element_type=F32)


def remote(src, dst, send, recv, device):
    return pltpu.make_async_remote_copy(
        src_ref=src,
        dst_ref=dst,
        send_sem=send,
        recv_sem=recv,
        device_id=device,
        device_id_type=MESH,
    )


def drain(ref, sem):
    pltpu.make_async_copy(ref, ref, sem).wait()


def kernel(
    dims,
    tok_ref,
    par_ref,
    up_hbm,
    down_hbm,
    cot_ref,
    mixed_ref,
    gtok_ref,
    gpar_ref,
    up,
    down,
    w_sem,
    par_sc,
    lg_part,
    lg_r1,
    lg_s1,
    lg_r2,
    lg_full,
    lg_send,
    lg_recv,
    disp,
    comb,
    disp_bf,
    comb_bf,
    stage,
    x_a,
    z_a,
    r_a,
    x_b,
    z_b,
    r_b,
    a2a_send,
    a2a_recv,
    rows,
    rows_send,
    rows_recv,
    preact,
    act,
    part,
    part_in,
    pair,
    pair_in,
    rs_send,
    rs_recv,
    slot,
    g_part,
    g_r1,
    g_s1,
    g_r2,
    g_full,
    g_send,
    g_recv,
    p0,
    p1,
    q0,
    q1,
    u0,
    u1,
    v0,
    v1,
    p_send,
    p_recv,
):
    ny, nx, nz, zl = dims
    zh = nz // zl
    nyx = ny * nx
    experts = nyx * nz
    feat = tok_ref.shape[1]
    lanes = feat // 2
    y, x, z = lax.axis_index("y"), lax.axis_index("x_lo"), lax.axis_index("z")
    xh, core = lax.axis_index("x_hi"), lax.axis_index("core")
    yx = y * nx + x
    own = xh * 2 + core
    across = (1 - xh) * 2 + core
    partner = {"core": 1 - core}
    cross = {"x_hi": 1 - xh}

    def yx_peer(step):
        peer = lax.rem(yx + step, nyx)
        return peer, {"y": peer // nx, "x_lo": lax.rem(peer, nx)}

    def z_peer(step):
        peer = lax.rem(z + step, nz)
        return peer, {"z": peer}

    barrier = pltpu.get_barrier_semaphore()

    def greet(device):
        pl.semaphore_signal(barrier, inc=1, device_id=device, device_id_type=MESH)

    greet(partner)
    greet(cross)
    lax.fori_loop(1, nz, lambda d, _: greet(z_peer(d)[1]), None)
    lax.fori_loop(1, nyx, lambda d, _: greet(yx_peer(d)[1]), None)
    load_up = pltpu.make_async_copy(up_hbm, up, w_sem.at[0])
    load_down = pltpu.make_async_copy(down_hbm, down, w_sem.at[1])
    load_up.start()
    load_down.start()

    columns = 2 * experts
    row_id = lax.broadcasted_iota(jnp.int32, (columns, columns), 0)
    col_id = lax.broadcasted_iota(jnp.int32, (columns, columns), 1)
    order = jnp.where(
        col_id == lax.rem(row_id, 2) * experts + row_id // 2, 1.0, 0.0
    ).astype(BF16)
    tok = tok_ref[...]
    par_sc[...] = dot(par_ref[...], order, 1, 0).astype(BF16)
    logits = dot(tok, par_sc[...], 1, 0)
    lg_part[0] = logits[:, :experts]
    lg_part[1] = logits[:, experts:]

    pl.semaphore_wait(barrier, nz + nyx)

    send0 = remote(lg_part.at[1 - core], lg_r1, lg_send.at[0], lg_recv.at[0], partner)
    send0.start()
    send0.wait_recv()
    lg_s1[...] = lg_part[core] + lg_r1[...]
    send1 = remote(lg_s1, lg_r2, lg_send.at[1], lg_recv.at[1], cross)
    send1.start()
    send1.wait_recv()
    lg_full[core] = lg_s1[...] + lg_r2[...]
    send2 = remote(lg_full.at[core], lg_full.at[core], lg_send.at[2], lg_recv.at[2], partner)
    send2.start()
    send2.wait_recv()

    top = jnp.maximum(
        jnp.max(lg_full[0], axis=1, keepdims=True), jnp.max(lg_full[1], axis=1, keepdims=True)
    )
    total = jnp.zeros_like(top)
    for s in range(2):
        e = jnp.exp(lg_full[s] - top)
        comb[s] = e
        total = total + jnp.sum(e, axis=1, keepdims=True)
        w = jnp.exp(lg_full[s] - jnp.max(lg_full[s], axis=0, keepdims=True))
        w = w / jnp.sum(w, axis=0, keepdims=True)
        disp[s] = w
        disp_bf[s] = w.astype(BF16)
    for s in range(2):
        c = comb[s] / total
        comb[s] = c
        comb_bf[s] = c.astype(BF16)

    def interleave(get, out):
        for a in range(2):
            for s in range(2):
                value = get(a, s)
                for k in range(2):
                    stage[pl.ds(a * 4 + s * 2 + k, experts, stride=8), :] = value[
                        :, k * lanes : (k + 1) * lanes
                    ]
        for i in range(nyx):
            block = stage[i * nz * 8 : (i + 1) * nz * 8, :]
            out[i] = block.reshape(nz, 8, lanes).astype(BF16)

    def deinterleave(source, put):
        for i in range(nyx):
            block = source[i].astype(F32)
            stage[i * nz * 8 : (i + 1) * nz * 8, :] = block.reshape(nz * 8, lanes)
        for a in range(2):
            for s in range(2):
                for k in range(2):
                    piece = stage[pl.ds(a * 4 + s * 2 + k, experts, stride=8), :]
                    put(a, s, k, piece.astype(BF16))

    def exchange(src, mid, dst, which):
        s0, r0 = a2a_send.at[which, 0], a2a_recv.at[which, 0]
        s1, r1 = a2a_send.at[which, 1], a2a_recv.at[which, 1]

        def z_send(step, _):
            peer, device = z_peer(step)
            remote(src.at[:, peer], mid.at[z], s0, r0, device).start()

        lax.fori_loop(1, nz, z_send, None)
        pltpu.make_async_copy(src.at[:, z], mid.at[z], r0).start()
        drain(mid, r0)

        def yx_send(step, _):
            peer, device = yx_peer(step)
            remote(mid.at[:, peer], dst.at[yx], s1, r1, device).start()

        lax.fori_loop(1, nyx, yx_send, None)
        pltpu.make_async_copy(mid.at[:, yx], dst.at[yx], r1).start()
        drain(dst, r1)

    def slot_rows(a, s):
        if a == 0:
            return dot(disp_bf[s], tok, 0, 0)
        return dot(comb_bf[s], cot_ref[...], 0, 0)

    interleave(slot_rows, x_a)
    exchange(x_a, z_a, r_a, 0)

    def put_rows(a, s, k, piece):
        rows[own, a, s * experts : (s + 1) * experts, k * lanes : (k + 1) * lanes] = piece

    deinterleave(r_a, put_rows)

    to_cross, to_partner, forward = [], [], []
    for a in range(2):
        mine = rows.at[own, a]
        to_cross.append(remote(mine, mine, rows_send.at[0, a], rows_recv.at[0, a], cross))
        to_partner.append(remote(mine, mine, rows_send.at[1, a], rows_recv.at[1, a], partner))
        to_cross[a].start()
        to_partner[a].start()
    for a in range(2):
        to_cross[a].wait_recv()
        got = rows.at[across, a]
        forward.append(remote(got, got, rows_send.at[2, a], rows_recv.at[2, a], partner))
        forward[a].start()
    for a in range(2):
        to_partner[a].wait_recv()
        forward[a].wait_recv()
    load_up.wait()
    load_down.wait()

    hidden = up.shape[1]
    width = hidden // 4

    def up_step(j, _):
        cols = pl.ds(pl.multiple_of(j * width, width), width)
        acc = jnp.zeros((columns, width), F32)
        for q in range(4):
            acc = acc + dot(rows[q, 0], up[q * feat : (q + 1) * feat, cols], 1, 0)
        preact[:, cols] = acc
        t = jnp.tanh(GELU_C * (acc + GELU_A * acc * acc * acc))
        act[0, :, cols] = (0.5 * acc * (1.0 + t)).astype(BF16)

    lax.fori_loop(0, 4, up_step, None)

    def grad_step(j, _):
        cols = pl.ds(pl.multiple_of(j * width, width), width)
        acc = jnp.zeros((columns, width), F32)
        for q in range(4):
            acc = acc + dot(rows[q, 1], down[cols, q * feat : (q + 1) * feat], 1, 1)
        v = preact[:, cols]
        t = jnp.tanh(GELU_C * (v + GELU_A * v * v * v))
        slope = 0.5 * (1.0 + t) + 0.5 * v * (1.0 - t * t) * (
            GELU_C * (1.0 + 3.0 * GELU_A * v * v)
        )
        act[1, :, cols] = (acc * slope).astype(BF16)

    lax.fori_loop(0, 4, grad_step, None)

    def out_step(j, _):
        cols = pl.ds(pl.multiple_of(j * feat, feat), feat)
        part[j, 0] = dot(act[0], down[:, cols], 1, 0).astype(BF16)
        part[j, 1] = dot(act[1], up[cols, :], 1, 1).astype(BF16)

    lax.fori_loop(0, 4, out_step, None)

    for i in range(2):
        remote(
            part.at[i * 2 + 1 - core], part_in.at[i], rs_send.at[0], rs_recv.at[0], partner
        ).start()
    drain(part_in, rs_recv.at[0])
    for a in range(2):
        pair[a] = (part[across, a].astype(F32) + part_in[1 - xh, a].astype(F32)).astype(BF16)
    send_pair = remote(pair, pair_in, rs_send.at[1], rs_recv.at[1], cross)
    send_pair.start()
    send_pair.wait_recv()

    def slot_result(a, s):
        r = slice(s * experts, (s + 1) * experts)
        kept = part[own, a, r, :].astype(F32) + part_in[xh, a, r, :].astype(F32)
        return kept + pair_in[a, r, :].astype(F32)

    interleave(slot_result, x_b)
    exchange(x_b, z_b, r_b, 1)

    def put_slot(a, s, k, piece):
        slot[a, s, :, k * lanes : (k + 1) * lanes] = piece

    deinterleave(r_b, put_slot)

    for s in range(2):
        g_part[s, 0] = dot(cot_ref[...], slot[0, s], 1, 1).astype(BF16)
        g_part[s, 1] = dot(tok, slot[1, s], 1, 1).astype(BF16)
    send3 = remote(g_part.at[1 - core], g_r1, g_send.at[0], g_recv.at[0], partner)
    send3.start()
    send3.wait_recv()
    g_s1[...] = (g_part[core].astype(F32) + g_r1[...].astype(F32)).astype(BF16)
    send4 = remote(g_s1, g_r2, g_send.at[1], g_recv.at[1], cross)
    send4.start()
    mixed = dot(comb_bf[0], slot[0, 0], 1, 0) + dot(comb_bf[1], slot[0, 1], 1, 0)
    mixed_ref[...] = mixed.astype(BF16)
    token_term = dot(disp_bf[0], slot[1, 0], 1, 0) + dot(disp_bf[1], slot[1, 1], 1, 0)
    send4.wait_recv()
    g_full[core] = (g_s1[...].astype(F32) + g_r2[...].astype(F32)).astype(BF16)
    send5 = remote(g_full.at[core], g_full.at[core], g_send.at[2], g_recv.at[2], partner)
    send5.start()
    send5.wait_recv()

    inner = jnp.zeros_like(top)
    for s in range(2):
        inner = inner + jnp.sum(comb[s] * g_full[s, 0].astype(F32), axis=1, keepdims=True)
    natural = jnp.zeros((tok.shape[0], columns), F32)
    for s in range(2):
        gd = g_full[s, 1].astype(F32)
        through = disp[s] * (gd - jnp.sum(disp[s] * gd, axis=0, keepdims=True))
        gl = (comb[s] * (g_full[s, 0].astype(F32) - inner) + through).astype(BF16)
        half = slice(s * experts, (s + 1) * experts)
        token_term = token_term + dot(gl, par_sc[:, half], 1, 1)
        natural = natural + dot(gl, order[:, half], 1, 1)
    gtok_ref[...] = token_term.astype(BF16)

    gpar = dot(tok, natural.astype(BF16), 0, 0)
    piece = feat // nyx
    for i in range(nyx):
        p0[i] = gpar[i * piece : (i + 1) * piece, :].astype(BF16)

    def scatter(step, _):
        peer, device = yx_peer(step)
        remote(p0.at[peer], p1.at[yx], p_send.at[0], p_recv.at[0], device).start()

    lax.fori_loop(1, nyx, scatter, None)
    pltpu.make_async_copy(p0.at[yx], p1.at[yx], p_recv.at[0]).start()
    drain(p1, p_recv.at[0])

    def summed(ref, count):
        value = ref[0].astype(F32)
        for i in range(1, count):
            value = value + ref[i].astype(F32)
        return value

    low, high = lax.rem(z, zl), z // zl
    q0[...] = summed(p1, nyx).astype(BF16)

    def share_low(step, _):
        peer = high * zl + lax.rem(low + step, zl)
        remote(q0, q1.at[low], p_send.at[1], p_recv.at[1], {"z": peer}).start()

    lax.fori_loop(1, zl, share_low, None)
    pltpu.make_async_copy(q0, q1.at[low], p_recv.at[1]).start()
    drain(q1, p_recv.at[1])
    u0[...] = summed(q1, zl).astype(BF16)

    def share_high(step, _):
        peer = lax.rem(high + step, zh) * zl + low
        remote(u0, u1.at[high], p_send.at[2], p_recv.at[2], {"z": peer}).start()

    lax.fori_loop(1, zh, share_high, None)
    pltpu.make_async_copy(u0, u1.at[high], p_recv.at[2]).start()
    drain(u1, p_recv.at[2])
    v0[...] = summed(u1, zh)

    def gather(step, _):
        _, device = yx_peer(step)
        remote(v0, v1.at[yx], p_send.at[3], p_recv.at[3], device).start()

    lax.fori_loop(1, nyx, gather, None)
    pltpu.make_async_copy(v0, v1.at[yx], p_recv.at[3]).start()
    drain(v1, p_recv.at[3])
    gpar_ref[...] = v1[...]

    for copy in (send0, send1, send2, send3, send4, send5, send_pair):
        copy.wait_send()
    for a in range(2):
        to_cross[a].wait_send()
        to_partner[a].wait_send()
        forward[a].wait_send()
    drain(part_in, rs_send.at[0])
    for which, mid, dst in ((0, z_a, r_a), (1, z_b, r_b)):
        drain(mid.at[pl.ds(0, nz - 1)], a2a_send.at[which, 0])
        if nyx > 1:
            drain(dst.at[pl.ds(0, nyx - 1)], a2a_send.at[which, 1])
    if nyx > 1:
        drain(p1.at[pl.ds(0, nyx - 1)], p_send.at[0])
        drain(v1.at[pl.ds(0, nyx - 1)], p_send.at[3])
    if zl > 1:
        drain(q1.at[pl.ds(0, zl - 1)], p_send.at[1])
    if zh > 1:
        drain(u1.at[pl.ds(0, zh - 1)], p_send.at[2])


def layer(dims, tokens, slot_params, w_up, w_down, cotangent):
    ny, nx, nz, zl = dims
    nyx, zh = ny * nx, nz // zl
    experts = nyx * nz
    seq, feat = tokens.shape
    columns = slot_params.shape[1]
    depth, hidden = w_up.shape[1:]
    lanes = feat // 2
    vmem, dma = pltpu.VMEM, pltpu.SemaphoreType.DMA
    piece = feat // nyx
    tile = (8, lanes)
    scratch = [
        vmem((depth, hidden), BF16),
        vmem((hidden, depth), BF16),
        dma((2,)),
        vmem((feat, columns), BF16),
        vmem((2, seq, experts), F32),
        vmem((seq, experts), F32),
        vmem((seq, experts), F32),
        vmem((seq, experts), F32),
        vmem((2, seq, experts), F32),
        dma((3,)),
        dma((3,)),
        vmem((2, seq, experts), F32),
        vmem((2, seq, experts), F32),
        vmem((2, seq, experts), BF16),
        vmem((2, seq, experts), BF16),
        vmem((8 * experts, lanes), F32),
    ]
    for _ in range(2):
        scratch += [
            vmem((nyx, nz) + tile, BF16),
            vmem((nz, nyx) + tile, BF16),
            vmem((nyx, nz) + tile, BF16),
        ]
    scratch += [
        dma((2, 2)),
        dma((2, 2)),
        vmem((4, 2, columns, feat), BF16),
        dma((3, 2)),
        dma((3, 2)),
        vmem((columns, hidden), F32),
        vmem((2, columns, hidden), BF16),
        vmem((4, 2, columns, feat), BF16),
        vmem((2, 2, columns, feat), BF16),
        vmem((2, columns, feat), BF16),
        vmem((2, columns, feat), BF16),
        dma((2,)),
        dma((2,)),
        vmem((2, 2, experts, feat), BF16),
        vmem((2, 2, seq, experts), BF16),
        vmem((2, seq, experts), BF16),
        vmem((2, seq, experts), BF16),
        vmem((2, seq, experts), BF16),
        vmem((2, 2, seq, experts), BF16),
        dma((3,)),
        dma((3,)),
        vmem((nyx, piece, columns), BF16),
        vmem((nyx, piece, columns), BF16),
        vmem((piece, columns), BF16),
        vmem((zl, piece, columns), BF16),
        vmem((piece, columns), BF16),
        vmem((zh, piece, columns), BF16),
        vmem((piece, columns), F32),
        vmem((nyx, piece, columns), F32),
        dma((4,)),
        dma((4,)),
    ]
    whole = pl.BlockSpec(memory_space=pltpu.VMEM)
    hbm = pl.BlockSpec(memory_space=pl.ANY)
    mixed, grad_tokens, grad_params = pl.pallas_call(
        functools.partial(kernel, dims),
        out_shape=(
            jax.ShapeDtypeStruct((seq, feat), BF16),
            jax.ShapeDtypeStruct((seq, feat), BF16),
            jax.ShapeDtypeStruct((nyx, piece, columns), F32),
        ),
        in_specs=[whole, whole, hbm, hbm, whole],
        out_specs=(whole, whole, whole),
        scratch_shapes=scratch,
        compiler_params=pltpu.CompilerParams(
            collective_id=0, has_side_effects=True, vmem_limit_bytes=48 << 20
        ),
    )(tokens, slot_params, w_up[0], w_down[0], cotangent)
    return mixed, grad_tokens, grad_params.reshape(feat, columns)


def build(mesh, dims):
    in_specs = (
        P(EXPERT, HALF),
        P(HALF, None),
        P(EXPERT, None, HALF),
        P(EXPERT, HALF, None),
        P(EXPERT, HALF),
    )
    out_specs = (P(EXPERT, HALF), P(EXPERT, HALF), P(HALF, None))
    return jax.shard_map(
        functools.partial(layer, dims),
        mesh=mesh,
        in_specs=in_specs,
        out_specs=out_specs,
        check_vma=False,
    )


def solution(mesh):
    return build(
        jax.sharding.Mesh(mesh.devices.reshape(4, 2, 16, 2, 2), EXPERT + HALF), (4, 2, 16, 4)
    )
```

time: 567 us -> 122 us (0.22)
  waiting for transfers between devices: 453 us -> 0 us
  Pallas kernels: 0 us -> 111 us
  starting transfers between devices: 46.9 us -> 0 us
  blocking collectives: 21.4 us -> 0 us
  matrix products: 14.1 us -> 0 us
  between operations: 14.5 us -> 0.65 us
  other arithmetic: 7.34 us -> 0 us
    psum x6 -> x0, waiting for transfers between devices: 403 us -> none  [the longest x3 238 us: local(): grad_params = lax.psum(lax.psum(lax.psum(params_part, 'z'), 'y'), 'x_lo')]
    pallas_call x0 -> x1, Pallas kernels: none -> 111 us  [layer(): pl.pallas_call(functools.partial(kernel, dims), out_shape=(jax.ShapeDtype...]
    all_to_all x4 -> x0, waiting for transfers between devices: 49.8 us -> none  [the longest x1 15.3 us: local(): lax.all_to_all(slot_in, EXPERT, split_axis=3, concat_axis=3, tiled=True)]
    all_to_all x4 -> x0, starting transfers between devices: 46.6 us -> none  [the longest x1 16.6 us: local(): lax.all_to_all(grad_slot_in.astype(jnp.bfloat16), EXPERT, split_axis=3, c...]
    all_gather x2 -> x0, blocking collectives: 21.4 us -> none  [the longest x1 11.5 us: local(): lax.all_gather(grad_received, HALF, axis=2, tiled=True)]
    dot_general x12 -> x0, matrix products: 14.1 us -> none  [the longest x1 4.51 us: local(): jnp.einsum('fk,sirk->fsir', up_slice, grad_preact, preferred_element_type...]
  transfers between devices with their start and end apart: 10 -> 0, of which waited for: 10 -> 0; matrix products, arithmetic and copies ran while one was open for 1% -> 0% of each run, Pallas kernels for 0% -> 0%
where the time goes in v2:
time: 122 us; the launch traced here: 119 us
  Pallas kernels  111 us (91%)
  local copies, waits for them, and re-layouts  7.85 us (6%)
    pallas_call x1, Pallas kernels, layer(): pl.pallas_call(functools.partial(kernel, dims), out_shape=(jax.ShapeDtype...  111 us
    unnamed x13, local copies, waits for them, and re-layouts  7.85 us

profile of v2, /device:TPU:1, one launch (start us, length us, event | category | flops | bytes accessed | tf_op | source)
XLA Modules:
  0.0 119.4 jit_solution(7722194633400396606)
XLA Ops:
  0.6 0.0 copy-start
  0.6 1.6 %copy-done = bf16[1,1024,1024]{2,1,0:T(8,128)(2,1)S(1)} copy-done((bf16[1,1024,1024]{2,1,0:T(8,128)(2,1)S(1)}, bf16[1,1024,1024]{2,1,0:T(8,128)(2,1)}, u32[]{:S(2)}) %copy-start) | copy-done | bytes 2097176
  2.2 0.0 copy-start.1
  2.2 1.6 %copy-done.1 = bf16[1,1024,1024]{2,1,0:T(8,128)(2,1)S(1)} copy-done((bf16[1,1024,1024]{2,1,0:T(8,128)(2,1)S(1)}, bf16[1,1024,1024]{2,1,0:T(8,128)(2,1)}, u32[]{:S(2)}) %copy-start.1) | copy-done | bytes 2097176
  3.8 0.0 copy-start.2
  3.8 0.9 copy-done.2
  4.7 0.0 copy-start.3
  4.7 0.9 copy-done.3
  5.6 0.0 copy-start.4
  5.6 0.9 copy-done.4
  6.5 110.8 %shard_map.76 = (bf16[196,256]{1,0:T(8,128)(2,1)S(1)}, bf16[196,256]{1,0:T(8,128)(2,1)S(1)}, f32[8,32,256]{2,1,0:T(8,128)S(1)}) custom-call(bf16[196,256]{1,0:T(8,128)(2,1)S(1)} %copy-done.3, bf16[256,256]{1,0:T(8,128)(2,1)S(1)} %copy-done.2, bf16[1024,1024]{1,0:T(8,128)(2,1)S(1)} %bitcast.3, bf16[1024,1024]{1,0:T(8,128)(2,1)S(1)} %bitcast.4, ...), custom_call_target="tpu_custom_call" | custom-call | tf_op jit(solution)/shard_map/pallas_call | solution.py:484
  117.4 0.6 copy.11
  118.0 0.6 copy.12
  118.7 0.7 copy.13
Async XLA Ops:
  0.6 1.6 %copy-start = (bf16[1,1024,1024]{2,1,0:T(8,128)(2,1)S(1)}, bf16[1,1024,1024]{2,1,0:T(8,128)(2,1)}, u32[]{:S(2)}) copy-start(bf16[1,1024,1024]{2,1,0:T(8,128)(2,1)} %param.7) | copy-start | bytes 6291460
  2.2 1.6 %copy-start.1 = (bf16[1,1024,1024]{2,1,0:T(8,128)(2,1)S(1)}, bf16[1,1024,1024]{2,1,0:T(8,128)(2,1)}, u32[]{:S(2)}) copy-start(bf16[1,1024,1024]{2,1,0:T(8,128)(2,1)} %param.8) | copy-start | bytes 6291460
  3.8 0.9 copy-start.2
  4.7 0.9 copy-start.3
  5.6 0.9 copy-start.4

commit v3 on v2

v3 whole, which is shorter than its diff:
```python
import functools

import jax
import jax.numpy as jnp
from jax import lax
from jax.experimental import pallas as pl
from jax.experimental.pallas import tpu as pltpu
from jax.sharding import PartitionSpec as P

SEQ = 196
BF16 = jnp.bfloat16
F32 = jnp.float32
EXPERT = ("y", "x_lo", "z")
HALF = ("x_hi", "core")
MESH = pl.DeviceIdType.MESH
GELU_C = 0.7978845608
GELU_A = 0.044715


def dot(a, b, ca, cb):
    return lax.dot_general(a, b, (((ca,), (cb,)), ((), ())), preferred_element_type=F32)


def remote(src, dst, send, recv, device):
    return pltpu.make_async_remote_copy(
        src_ref=src,
        dst_ref=dst,
        send_sem=send,
        recv_sem=recv,
        device_id=device,
        device_id_type=MESH,
    )


def drain(ref, sem):
    pltpu.make_async_copy(ref, ref, sem).wait()


def kernel(
    dims,
    tok_hbm,
    par_hbm,
    up_hbm,
    down_hbm,
    cot_hbm,
    mixed_hbm,
    gtok_hbm,
    gpar_hbm,
    tok_ref,
    par_ref,
    cot_ref,
    up,
    down,
    in_sem,
    mixed_ref,
    gtok_ref,
    gpar_ref,
    out_sem,
    par_sc,
    lg_part,
    lg_r1,
    lg_s1,
    lg_r2,
    lg_full,
    lg_send,
    lg_recv,
    disp,
    comb,
    disp_bf,
    comb_bf,
    stage,
    x_buf,
    z_buf,
    r_buf,
    a2a_send,
    a2a_recv,
    rows,
    rows_send,
    rows_recv,
    preact,
    act,
    part,
    part_in,
    pair,
    pair_in,
    rs_send,
    rs_recv,
    slot,
    g_part,
    g_r1,
    g_s1,
    g_r2,
    g_full,
    g_send,
    g_recv,
    p0,
    p1,
    q0,
    q1,
    u0,
    u1,
    v0,
    v1,
    p_send,
    p_recv,
    know_x,
    know_y,
    know_z,
):
    ny, nx, nz, zl = dims
    zh = nz // zl
    nyx = ny * nx
    experts = nyx * nz
    feat = tok_ref.shape[1]
    lanes = feat // 2
    y, x, z = lax.axis_index("y"), lax.axis_index("x_lo"), lax.axis_index("z")
    xh, core = lax.axis_index("x_hi"), lax.axis_index("core")
    yx = y * nx + x
    own = xh * 2 + core
    across = (1 - xh) * 2 + core
    partner = {"core": 1 - core}
    cross = {"x_hi": 1 - xh}
    sent = []

    def start(src, dst, send, recv, device):
        copy = remote(src, dst, send, recv, device)
        copy.start()
        sent.append(copy)
        return copy

    moves = [(dy, dx) for dy in range(ny) for dx in range(nx) if dy + dx]
    moves.sort(key=lambda m: -min(m[0], ny - m[0]) - min(m[1], nx - m[1]))

    def yx_each(action):
        for dy, dx in moves:
            py, px = lax.rem(y + dy, ny), lax.rem(x + dx, nx)
            action(py * nx + px, {"y": py, "x_lo": px})

    def z_peer(step):
        swing = step // 2
        ahead = nz // 2 + jnp.where(lax.rem(step, 2) == 0, -swing, swing)
        peer = lax.rem(z + ahead, nz)
        return peer, {"z": peer}

    loads = []
    for i, (src, dst) in enumerate(
        (
            (tok_hbm, tok_ref),
            (par_hbm, par_ref),
            (cot_hbm, cot_ref),
            (up_hbm, up),
            (down_hbm, down),
        )
    ):
        loads.append(pltpu.make_async_copy(src, dst, in_sem.at[i]))
        loads[i].start()
    barrier = pltpu.get_barrier_semaphore()

    def greet(device):
        pl.semaphore_signal(barrier, inc=1, device_id=device, device_id_type=MESH)

    def z_near(step):
        return [{"z": lax.rem(z + step, nz)}, {"z": lax.rem(z + nz - step, nz)}]

    y_near = [{"y": lax.rem(y + 1, ny)}, {"y": lax.rem(y + ny - 1, ny)}]
    x_near = {"x_lo": lax.rem(x + 1, nx)}
    near = [partner, cross, x_near] + y_near + z_near(1)
    for device in near:
        greet(device)

    def tell(sem, devices):
        for device in devices:
            pl.semaphore_signal(sem, inc=1, device_id=device, device_id_type=MESH)

    columns = 2 * experts
    row_id = lax.broadcasted_iota(jnp.int32, (columns, columns), 0)
    col_id = lax.broadcasted_iota(jnp.int32, (columns, columns), 1)
    order = jnp.where(
        col_id == lax.rem(row_id, 2) * experts + row_id // 2, 1.0, 0.0
    ).astype(BF16)
    loads[0].wait()
    loads[1].wait()
    tok = tok_ref[...]
    par_sc[...] = dot(par_ref[...], order, 1, 0).astype(BF16)
    logits = dot(tok, par_sc[...], 1, 0)
    lg_part[0] = logits[:, :experts]
    lg_part[1] = logits[:, experts:]

    pl.semaphore_wait(barrier, len(near))
    tell(know_z.at[0], z_near(1))
    tell(know_y, y_near)

    start(lg_part.at[1 - core], lg_r1, lg_send.at[0], lg_recv.at[0], partner).wait_recv()
    lg_s1[...] = lg_part[core] + lg_r1[...]
    summed_over = start(lg_s1, lg_r2, lg_send.at[1], lg_recv.at[1], cross)
    pl.semaphore_wait(know_z.at[0], 2)
    tell(know_z.at[1], z_near(2))
    pl.semaphore_wait(know_y, 2)
    tell(know_x, [x_near])
    pl.semaphore_wait(know_z.at[1], 2)
    tell(know_z.at[2], z_near(4))
    summed_over.wait_recv()
    lg_full[core] = lg_s1[...] + lg_r2[...]
    mine = lg_full.at[core]
    start(mine, mine, lg_send.at[2], lg_recv.at[2], partner).wait_recv()

    def interleave(get, out):
        for s in range(2):
            value = get(s)
            for k in range(2):
                stage[pl.ds(s * 2 + k, experts, stride=8), :] = value[
                    :, k * lanes : (k + 1) * lanes
                ]
        for i in range(nyx):
            block = stage[i * nz * 8 : (i + 1) * nz * 8, :].reshape(nz, 8, lanes)
            out[:, i] = block[:, :4, :].astype(BF16)

    def deinterleave(source, put):
        fill = jnp.zeros((nz, 4, lanes), F32)
        for i in range(nyx):
            block = jnp.concatenate([source[i].astype(F32), fill], axis=1)
            stage[i * nz * 8 : (i + 1) * nz * 8, :] = block.reshape(nz * 8, lanes)
        for s in range(2):
            for k in range(2):
                piece = stage[pl.ds(s * 2 + k, experts, stride=8), :]
                put(s, k, piece.astype(BF16))

    def z_start(trip, a):
        src, mid = x_buf.at[trip, a], z_buf.at[trip, a]
        s0, r0 = a2a_send.at[trip, a, 0], a2a_recv.at[trip, a, 0]

        def z_send(step, _):
            peer, device = z_peer(step)
            remote(src.at[peer], mid.at[z], s0, r0, device).start()

        lax.fori_loop(1, nz, z_send, None)
        pltpu.make_async_copy(src.at[z], mid.at[z], r0).start()

    def yx_start(trip, a):
        mid, dst = z_buf.at[trip, a], r_buf.at[trip, a]
        s1, r1 = a2a_send.at[trip, a, 1], a2a_recv.at[trip, a, 1]
        drain(mid, a2a_recv.at[trip, a, 0])

        def yx_send(peer, device):
            remote(mid.at[:, peer], dst.at[yx], s1, r1, device).start()

        yx_each(yx_send)
        pltpu.make_async_copy(mid.at[:, yx], dst.at[yx], r1).start()

    def yx_wait(trip, a):
        drain(r_buf.at[trip, a], a2a_recv.at[trip, a, 1])

    pl.semaphore_wait(know_x, 1)
    pl.semaphore_wait(know_z.at[2], 2)
    for s in range(2):
        w = jnp.exp(lg_full[s] - jnp.max(lg_full[s], axis=0, keepdims=True))
        w = w / jnp.sum(w, axis=0, keepdims=True)
        disp[s] = w
        disp_bf[s] = w.astype(BF16)
    interleave(lambda s: dot(disp_bf[s], tok, 0, 0), x_buf.at[0, 0])
    z_start(0, 0)
    top = jnp.maximum(
        jnp.max(lg_full[0], axis=1, keepdims=True), jnp.max(lg_full[1], axis=1, keepdims=True)
    )
    total = jnp.zeros_like(top)
    for s in range(2):
        e = jnp.exp(lg_full[s] - top)
        comb[s] = e
        total = total + jnp.sum(e, axis=1, keepdims=True)
    for s in range(2):
        c = comb[s] / total
        comb[s] = c
        comb_bf[s] = c.astype(BF16)
    loads[2].wait()
    interleave(lambda s: dot(comb_bf[s], cot_ref[...], 0, 0), x_buf.at[0, 1])
    z_start(0, 1)

    def put_rows(a):
        def put(s, k, piece):
            rows[own, a, s * experts : (s + 1) * experts, k * lanes : (k + 1) * lanes] = piece

        return put

    def ag_start(a):
        mine = rows.at[own, a]
        start(mine, mine, rows_send.at[0, a], rows_recv.at[0, a], cross)
        start(mine, mine, rows_send.at[1, a], rows_recv.at[1, a], partner)

    def ag_forward(a):
        got = rows.at[across, a]
        drain(got, rows_recv.at[0, a])
        start(got, got, rows_send.at[2, a], rows_recv.at[2, a], partner)

    def ag_wait(a):
        drain(rows.at[0, a], rows_recv.at[1, a])
        drain(rows.at[0, a], rows_recv.at[2, a])

    hidden = up.shape[1]
    width = hidden // 4

    def up_step(j, _):
        cols = pl.ds(pl.multiple_of(j * width, width), width)
        acc = jnp.zeros((columns, width), F32)
        for q in range(4):
            acc = acc + dot(rows[q, 0], up[q * feat : (q + 1) * feat, cols], 1, 0)
        preact[:, cols] = acc
        t = jnp.tanh(GELU_C * (acc + GELU_A * acc * acc * acc))
        act[0, :, cols] = (0.5 * acc * (1.0 + t)).astype(BF16)

    def grad_step(j, _):
        cols = pl.ds(pl.multiple_of(j * width, width), width)
        acc = jnp.zeros((columns, width), F32)
        for q in range(4):
            acc = acc + dot(rows[q, 1], down[cols, q * feat : (q + 1) * feat], 1, 1)
        v = preact[:, cols]
        t = jnp.tanh(GELU_C * (v + GELU_A * v * v * v))
        slope = 0.5 * (1.0 + t) + 0.5 * v * (1.0 - t * t) * (
            GELU_C * (1.0 + 3.0 * GELU_A * v * v)
        )
        act[1, :, cols] = (acc * slope).astype(BF16)

    def quarter(a, j):
        cols = pl.ds(pl.multiple_of(j * feat, feat), feat)
        if a == 0:
            value = dot(act[0], down[:, cols], 1, 0)
        else:
            value = dot(act[1], up[cols, :], 1, 1)
        part[a, j] = value.astype(BF16)

    def rs_start(a):
        for i, half in enumerate((1 - xh, xh)):
            quarter(a, half * 2 + 1 - core)
            start(
                part.at[a, half * 2 + 1 - core],
                part_in.at[a, i],
                rs_send.at[i, a],
                rs_recv.at[i, a],
                partner,
            )
        quarter(a, across)
        quarter(a, own)

    def rs_pair(a):
        drain(part_in.at[a, 0], rs_recv.at[0, a])
        pair[a] = (part[a, across].astype(F32) + part_in[a, 0].astype(F32)).astype(BF16)
        start(pair.at[a], pair_in.at[a], rs_send.at[2, a], rs_recv.at[2, a], cross)

    def rs_finish(a):
        drain(part_in.at[a, 1], rs_recv.at[1, a])
        drain(pair_in.at[a], rs_recv.at[2, a])

        def result(s):
            r = slice(s * experts, (s + 1) * experts)
            kept = part[a, own, r, :].astype(F32) + part_in[a, 1, r, :].astype(F32)
            return kept + pair_in[a, r, :].astype(F32)

        interleave(result, x_buf.at[1, a])
        z_start(1, a)

    yx_start(0, 0)
    yx_wait(0, 0)
    deinterleave(r_buf.at[0, 0], put_rows(0))
    ag_start(0)
    yx_start(0, 1)
    ag_forward(0)
    yx_wait(0, 1)
    deinterleave(r_buf.at[0, 1], put_rows(1))
    ag_start(1)
    ag_wait(0)
    loads[3].wait()
    lax.fori_loop(0, 4, up_step, None)
    loads[4].wait()
    ag_forward(1)
    rs_start(0)
    rs_pair(0)
    ag_wait(1)
    lax.fori_loop(0, 4, grad_step, None)
    rs_start(1)
    rs_pair(1)
    rs_finish(0)
    rs_finish(1)

    def put_slot(a):
        def put(s, k, piece):
            slot[a, s, :, k * lanes : (k + 1) * lanes] = piece

        return put

    def g_start(kind):
        start(g_part.at[kind, 1 - core], g_r1.at[kind], g_send.at[0, kind], g_recv.at[0, kind], partner)

    def g_pair(kind):
        drain(g_r1.at[kind], g_recv.at[0, kind])
        g_s1[kind] = (g_part[kind, core].astype(F32) + g_r1[kind].astype(F32)).astype(BF16)
        start(g_s1.at[kind], g_r2.at[kind], g_send.at[1, kind], g_recv.at[1, kind], cross)

    def g_share(kind):
        drain(g_r2.at[kind], g_recv.at[1, kind])
        g_full[kind, core] = (g_s1[kind].astype(F32) + g_r2[kind].astype(F32)).astype(BF16)
        mine = g_full.at[kind, core]
        start(mine, mine, g_send.at[2, kind], g_recv.at[2, kind], partner)

    def g_wait(kind):
        drain(g_full.at[kind, 0], g_recv.at[2, kind])

    yx_start(1, 0)
    yx_wait(1, 0)
    deinterleave(r_buf.at[1, 0], put_slot(0))
    for s in range(2):
        g_part[0, s] = dot(cot_ref[...], slot[0, s], 1, 1).astype(BF16)
    g_start(0)
    yx_start(1, 1)
    g_pair(0)
    mixed = dot(comb_bf[0], slot[0, 0], 1, 0) + dot(comb_bf[1], slot[0, 1], 1, 0)
    mixed_ref[...] = mixed.astype(BF16)
    store_mixed = pltpu.make_async_copy(mixed_ref, mixed_hbm, out_sem.at[0])
    store_mixed.start()
    yx_wait(1, 1)
    deinterleave(r_buf.at[1, 1], put_slot(1))
    for s in range(2):
        g_part[1, s] = dot(tok, slot[1, s], 1, 1).astype(BF16)
    g_start(1)
    g_share(0)
    g_pair(1)
    token_term = dot(disp_bf[0], slot[1, 0], 1, 0) + dot(disp_bf[1], slot[1, 1], 1, 0)
    g_wait(0)
    inner = jnp.zeros_like(top)
    for s in range(2):
        inner = inner + jnp.sum(comb[s] * g_full[0, s].astype(F32), axis=1, keepdims=True)
    for s in range(2):
        comb[s] = comb[s] * (g_full[0, s].astype(F32) - inner)
    g_share(1)
    g_wait(1)

    natural = jnp.zeros((tok.shape[0], columns), F32)
    grads = []
    for s in range(2):
        gd = g_full[1, s].astype(F32)
        through = disp[s] * (gd - jnp.sum(disp[s] * gd, axis=0, keepdims=True))
        grads.append((comb[s] + through).astype(BF16))
        half = slice(s * experts, (s + 1) * experts)
        natural = natural + dot(grads[s], order[:, half], 1, 1)

    gpar = dot(tok, natural.astype(BF16), 0, 0)
    piece = feat // nyx
    for i in range(nyx):
        p0[i] = gpar[i * piece : (i + 1) * piece, :].astype(BF16)

    def scatter(peer, device):
        remote(p0.at[peer], p1.at[yx], p_send.at[0], p_recv.at[0], device).start()

    yx_each(scatter)
    pltpu.make_async_copy(p0.at[yx], p1.at[yx], p_recv.at[0]).start()
    for s in range(2):
        half = slice(s * experts, (s + 1) * experts)
        token_term = token_term + dot(grads[s], par_sc[:, half], 1, 1)
    gtok_ref[...] = token_term.astype(BF16)
    store_gtok = pltpu.make_async_copy(gtok_ref, gtok_hbm, out_sem.at[1])
    store_gtok.start()
    drain(p1, p_recv.at[0])

    def summed(ref, count):
        value = ref[0].astype(F32)
        for i in range(1, count):
            value = value + ref[i].astype(F32)
        return value

    low, high = lax.rem(z, zl), z // zl
    q0[...] = summed(p1, nyx).astype(BF16)

    def share_low(step, _):
        peer = high * zl + lax.rem(low + step, zl)
        remote(q0, q1.at[low], p_send.at[1], p_recv.at[1], {"z": peer}).start()

    lax.fori_loop(1, zl, share_low, None)
    pltpu.make_async_copy(q0, q1.at[low], p_recv.at[1]).start()
    drain(q1, p_recv.at[1])
    u0[...] = summed(q1, zl).astype(BF16)

    def share_high(step, _):
        ahead = jnp.where(step == 1, zh // 2, jnp.where(step <= zh // 2, step - 1, step))
        peer = lax.rem(high + ahead, zh) * zl + low
        remote(u0, u1.at[high], p_send.at[2], p_recv.at[2], {"z": peer}).start()

    lax.fori_loop(1, zh, share_high, None)
    pltpu.make_async_copy(u0, u1.at[high], p_recv.at[2]).start()
    drain(u1, p_recv.at[2])
    v0[...] = summed(u1, zh).astype(BF16)

    def gather(_, device):
        remote(v0, v1.at[yx], p_send.at[3], p_recv.at[3], device).start()

    yx_each(gather)
    pltpu.make_async_copy(v0, v1.at[yx], p_recv.at[3]).start()
    drain(v1, p_recv.at[3])
    gpar_ref[...] = v1[...].astype(F32)
    store_gpar = pltpu.make_async_copy(gpar_ref, gpar_hbm, out_sem.at[2])
    store_gpar.start()

    for copy in sent:
        copy.wait_send()
    for trip in range(2):
        for a in range(2):
            drain(z_buf.at[trip, a, pl.ds(0, nz - 1)], a2a_send.at[trip, a, 0])
            if nyx > 1:
                drain(r_buf.at[trip, a, pl.ds(0, nyx - 1)], a2a_send.at[trip, a, 1])
    if nyx > 1:
        drain(p1.at[pl.ds(0, nyx - 1)], p_send.at[0])
        drain(v1.at[pl.ds(0, nyx - 1)], p_send.at[3])
    if zl > 1:
        drain(q1.at[pl.ds(0, zl - 1)], p_send.at[1])
    if zh > 1:
        drain(u1.at[pl.ds(0, zh - 1)], p_send.at[2])
    store_mixed.wait()
    store_gtok.wait()
    store_gpar.wait()


def publish(*refs):
    sources, targets, held, sem = refs[:3], refs[3:6], refs[6:9], refs[9]
    fetch = [pltpu.make_async_copy(sources[i], held[i], sem.at[0, i]) for i in range(3)]
    store = [pltpu.make_async_copy(held[i], targets[i], sem.at[1, i]) for i in range(3)]
    for copy in fetch:
        copy.start()
    for i in range(3):
        fetch[i].wait()
        store[i].start()
    for copy in store:
        copy.wait()


def layer(dims, tokens, slot_params, w_up, w_down, cotangent):
    ny, nx, nz, zl = dims
    nyx, zh = ny * nx, nz // zl
    experts = nyx * nz
    seq, feat = tokens.shape
    columns = slot_params.shape[1]
    depth, hidden = w_up.shape[1:]
    lanes = feat // 2
    vmem, dma = pltpu.VMEM, pltpu.SemaphoreType.DMA
    piece = feat // nyx
    scratch = [
        vmem((seq, feat), BF16),
        vmem((feat, columns), BF16),
        vmem((seq, feat), BF16),
        vmem((depth, hidden), BF16),
        vmem((hidden, depth), BF16),
        dma((5,)),
        vmem((seq, feat), BF16),
        vmem((seq, feat), BF16),
        vmem((nyx, piece, columns), F32),
        dma((3,)),
        vmem((feat, columns), BF16),
        vmem((2, seq, experts), F32),
        vmem((seq, experts), F32),
        vmem((seq, experts), F32),
        vmem((seq, experts), F32),
        vmem((2, seq, experts), F32),
        dma((3,)),
        dma((3,)),
        vmem((2, seq, experts), F32),
        vmem((2, seq, experts), F32),
        vmem((2, seq, experts), BF16),
        vmem((2, seq, experts), BF16),
        vmem((8 * experts, lanes), F32),
        vmem((2, 2, nz, nyx, 4, lanes), BF16),
        vmem((2, 2, nz, nyx, 4, lanes), BF16),
        vmem((2, 2, nyx, nz, 4, lanes), BF16),
        dma((2, 2, 2)),
        dma((2, 2, 2)),
        vmem((4, 2, columns, feat), BF16),
        dma((3, 2)),
        dma((3, 2)),
        vmem((columns, hidden), F32),
        vmem((2, columns, hidden), BF16),
        vmem((2, 4, columns, feat), BF16),
        vmem((2, 2, columns, feat), BF16),
        vmem((2, columns, feat), BF16),
        vmem((2, columns, feat), BF16),
        dma((3, 2)),
        dma((3, 2)),
        vmem((2, 2, experts, feat), BF16),
        vmem((2, 2, seq, experts), BF16),
        vmem((2, seq, experts), BF16),
        vmem((2, seq, experts), BF16),
        vmem((2, seq, experts), BF16),
        vmem((2, 2, seq, experts), BF16),
        dma((3, 2)),
        dma((3, 2)),
        vmem((nyx, piece, columns), BF16),
        vmem((nyx, piece, columns), BF16),
        vmem((piece, columns), BF16),
        vmem((zl, piece, columns), BF16),
        vmem((piece, columns), BF16),
        vmem((zh, piece, columns), BF16),
        vmem((piece, columns), BF16),
        vmem((nyx, piece, columns), BF16),
        dma((4,)),
        dma((4,)),
        pltpu.SemaphoreType.REGULAR,
        pltpu.SemaphoreType.REGULAR,
        pltpu.SemaphoreType.REGULAR((3,)),
    ]
    hbm = pl.BlockSpec(memory_space=pltpu.HBM)
    results = pl.pallas_call(
        functools.partial(kernel, dims),
        out_shape=(
            jax.ShapeDtypeStruct((seq, feat), BF16),
            jax.ShapeDtypeStruct((seq, feat), BF16),
            jax.ShapeDtypeStruct((nyx, piece, columns), F32),
        ),
        in_specs=[hbm] * 5,
        out_specs=(hbm, hbm, hbm),
        scratch_shapes=scratch,
        compiler_params=pltpu.CompilerParams(
            collective_id=0, has_side_effects=True, vmem_limit_bytes=67043328
        ),
    )(tokens, slot_params, w_up[0], w_down[0], cotangent)
    mixed, grad_tokens, grad_params = pl.pallas_call(
        publish,
        out_shape=tuple(jax.ShapeDtypeStruct(r.shape, r.dtype) for r in results),
        in_specs=[hbm] * 3,
        out_specs=(hbm, hbm, hbm),
        scratch_shapes=[vmem(r.shape, r.dtype) for r in results] + [dma((2, 3))],
        compiler_params=pltpu.CompilerParams(vmem_limit_bytes=67043328),
    )(*results)
    return mixed, grad_tokens, grad_params.reshape(feat, columns)


def build(mesh, dims):
    in_specs = (
        P(EXPERT, HALF),
        P(HALF, None),
        P(EXPERT, None, HALF),
        P(EXPERT, HALF, None),
        P(EXPERT, HALF),
    )
    out_specs = (P(EXPERT, HALF), P(EXPERT, HALF), P(HALF, None))
    return jax.shard_map(
        functools.partial(layer, dims),
        mesh=mesh,
        in_specs=in_specs,
        out_specs=out_specs,
        check_vma=False,
    )


def solution(mesh):
    return build(
        jax.sharding.Mesh(mesh.devices.reshape(4, 2, 16, 2, 2), EXPERT + HALF), (4, 2, 16, 4)
    )
```

time: 122 us -> 102 us (0.84)
  the two profiles are of different devices: /device:TPU:1 before, /device:TPU:2 now
where the time goes in v3:
time: 102 us
  Pallas kernels  101 us (99%)
    pallas_call x1, Pallas kernels, layer(): pl.pallas_call(functools.partial(kernel, dims), out_shape=(jax.ShapeDtype...  99.1 us

profile of v3, /device:TPU:2, one launch (start us, length us, event | category | flops | bytes accessed | tf_op | source)
XLA Modules:
  0.0 101.5 jit_solution(3332704817334487184)
XLA Ops:
  0.6 99.1 %shard_map.76 = (bf16[196,256]{1,0:T(8,128)(2,1)}, bf16[196,256]{1,0:T(8,128)(2,1)}, f32[8,32,256]{2,1,0:T(8,128)}) custom-call(bf16[196,256]{1,0:T(8,128)(2,1)} %tok_hbm.1, bf16[256,256]{1,0:T(8,128)(2,1)} %par_hbm.1, bf16[1024,1024]{1,0:T(8,128)(2,1)} %bitcast.3, bf16[1024,1024]{1,0:T(8,128)(2,1)} %bitcast.4, bf16[196,256]{1,0:T(8,128)(2,1)} %cot_hbm.1), custom_call_target="tpu_custom_call" | custom-call | tf_op jit(solution)/shard_map/pallas_call | solution.py:605
  99.7 1.8 %shard_map.77 = (bf16[196,256]{1,0:T(8,128)(2,1)}, bf16[196,256]{1,0:T(8,128)(2,1)}, f32[8,32,256]{2,1,0:T(8,128)}) custom-call(bf16[196,256]{1,0:T(8,128)(2,1)} %get-tuple-element.9.refs_0_, bf16[196,256]{1,0:T(8,128)(2,1)} %get-tuple-element.10.refs_1_, f32[8,32,256]{2,1,0:T(8,128)} %get-tuple-element.11.refs_2_), custom_call_target="tpu_custom_call" | custom-call | tf_op jit(solution)/shard_map/pallas_call | solution.py:619

commit v4 on v3

--- a/solution.py
+++ b/solution.py
@@ -72,6 +72,8 @@
     x_buf,
     z_buf,
     r_buf,
+    back_buf,
+    w_buf,
     a2a_send,
     a2a_recv,
     rows,
@@ -81,8 +83,6 @@
     act,
     part,
     part_in,
-    pair,
-    pair_in,
     rs_send,
     rs_recv,
     slot,
@@ -164,7 +164,8 @@
 
     y_near = [{"y": lax.rem(y + 1, ny)}, {"y": lax.rem(y + ny - 1, ny)}]
     x_near = {"x_lo": lax.rem(x + 1, nx)}
-    near = [partner, cross, x_near] + y_near + z_near(1)
+    x_ring = [x_near, cross, {"x_lo": 1 - x, "x_hi": 1 - xh}]
+    near = [partner] + x_ring + y_near + z_near(1)
     for device in near:
         greet(device)
 
@@ -196,7 +197,7 @@
     pl.semaphore_wait(know_z.at[0], 2)
     tell(know_z.at[1], z_near(2))
     pl.semaphore_wait(know_y, 2)
-    tell(know_x, [x_near])
+    tell(know_x, x_ring)
     pl.semaphore_wait(know_z.at[1], 2)
     tell(know_z.at[2], z_near(4))
     summed_over.wait_recv()
@@ -204,7 +205,7 @@
     mine = lg_full.at[core]
     start(mine, mine, lg_send.at[2], lg_recv.at[2], partner).wait_recv()
 
-    def interleave(get, out):
+    def interleave(get, out, by_z):
         for s in range(2):
             value = get(s)
             for k in range(2):
@@ -213,12 +214,16 @@
                 ]
         for i in range(nyx):
             block = stage[i * nz * 8 : (i + 1) * nz * 8, :].reshape(nz, 8, lanes)
-            out[:, i] = block[:, :4, :].astype(BF16)
-
-    def deinterleave(source, put):
+            if by_z:
+                out[:, i] = block[:, :4, :].astype(BF16)
+            else:
+                out[i] = block[:, :4, :].astype(BF16)
+
+    def deinterleave(source, put, by_z):
         fill = jnp.zeros((nz, 4, lanes), F32)
         for i in range(nyx):
-            block = jnp.concatenate([source[i].astype(F32), fill], axis=1)
+            block = source[:, i] if by_z else source[i]
+            block = jnp.concatenate([block.astype(F32), fill], axis=1)
             stage[i * nz * 8 : (i + 1) * nz * 8, :] = block.reshape(nz * 8, lanes)
         for s in range(2):
             for k in range(2):
@@ -226,7 +231,7 @@
                 put(s, k, piece.astype(BF16))
 
     def z_start(trip, a):
-        src, mid = x_buf.at[trip, a], z_buf.at[trip, a]
+        src, mid = (x_buf if trip == 0 else w_buf).at[a], z_buf.at[trip, a]
         s0, r0 = a2a_send.at[trip, a, 0], a2a_recv.at[trip, a, 0]
 
         def z_send(step, _):
@@ -236,28 +241,33 @@
         lax.fori_loop(1, nz, z_send, None)
         pltpu.make_async_copy(src.at[z], mid.at[z], r0).start()
 
-    def yx_start(trip, a):
-        mid, dst = z_buf.at[trip, a], r_buf.at[trip, a]
+    def z_wait(trip, a):
+        drain(z_buf.at[trip, a], a2a_recv.at[trip, a, 0])
+
+    flips = [(dy, fx, fh) for dy in range(ny) for fx in range(nx) for fh in range(2)][1:]
+    flips.sort(key=lambda m: -min(m[0], ny - m[0]) - (m[1] if m[1] else 2 * m[2]))
+
+    def wide_start(trip, a, source):
+        dst = r_buf.at[trip, a, xh, yx]
         s1, r1 = a2a_send.at[trip, a, 1], a2a_recv.at[trip, a, 1]
-        drain(mid, a2a_recv.at[trip, a, 0])
-
-        def yx_send(peer, device):
-            remote(mid.at[:, peer], dst.at[yx], s1, r1, device).start()
-
-        yx_each(yx_send)
-        pltpu.make_async_copy(mid.at[:, yx], dst.at[yx], r1).start()
-
-    def yx_wait(trip, a):
+        for dy, fx, fh in flips:
+            py, px = lax.rem(y + dy, ny), (1 - x if fx else x)
+            ph = 1 - xh if fh else xh
+            device = {"y": py, "x_lo": px, "x_hi": ph}
+            remote(source(ph, py * nx + px), dst, s1, r1, device).start()
+        pltpu.make_async_copy(source(xh, yx), dst, r1).start()
+
+    def wide_wait(trip, a):
         drain(r_buf.at[trip, a], a2a_recv.at[trip, a, 1])
 
-    pl.semaphore_wait(know_x, 1)
+    pl.semaphore_wait(know_x, 3)
     pl.semaphore_wait(know_z.at[2], 2)
     for s in range(2):
         w = jnp.exp(lg_full[s] - jnp.max(lg_full[s], axis=0, keepdims=True))
         w = w / jnp.sum(w, axis=0, keepdims=True)
         disp[s] = w
         disp_bf[s] = w.astype(BF16)
-    interleave(lambda s: dot(disp_bf[s], tok, 0, 0), x_buf.at[0, 0])
+    interleave(lambda s: dot(disp_bf[s], tok, 0, 0), x_buf.at[0], True)
     z_start(0, 0)
     top = jnp.maximum(
         jnp.max(lg_full[0], axis=1, keepdims=True), jnp.max(lg_full[1], axis=1, keepdims=True)
@@ -272,37 +282,41 @@
         comb[s] = c
         comb_bf[s] = c.astype(BF16)
     loads[2].wait()
-    interleave(lambda s: dot(comb_bf[s], cot_ref[...], 0, 0), x_buf.at[0, 1])
+    interleave(lambda s: dot(comb_bf[s], cot_ref[...], 0, 0), x_buf.at[1], True)
     z_start(0, 1)
 
-    def put_rows(a):
+    def put_rows(a, h):
         def put(s, k, piece):
-            rows[own, a, s * experts : (s + 1) * experts, k * lanes : (k + 1) * lanes] = piece
+            rows[a, core, h, s * experts : (s + 1) * experts, k * lanes : (k + 1) * lanes] = piece
 
         return put
 
-    def ag_start(a):
-        mine = rows.at[own, a]
-        start(mine, mine, rows_send.at[0, a], rows_recv.at[0, a], cross)
-        start(mine, mine, rows_send.at[1, a], rows_recv.at[1, a], partner)
-
-    def ag_forward(a):
-        got = rows.at[across, a]
-        drain(got, rows_recv.at[0, a])
-        start(got, got, rows_send.at[2, a], rows_recv.at[2, a], partner)
-
-    def ag_wait(a):
-        drain(rows.at[0, a], rows_recv.at[1, a])
-        drain(rows.at[0, a], rows_recv.at[2, a])
+    def share(a):
+        wide_wait(0, a)
+        for h in range(2):
+            deinterleave(r_buf.at[0, a, h], put_rows(a, h), False)
+        mine = rows.at[a, core]
+        start(mine, mine, rows_send.at[a], rows_recv.at[a], partner)
+
+    def share_wait(a):
+        drain(rows.at[a, 0], rows_recv.at[a])
 
     hidden = up.shape[1]
     width = hidden // 4
 
+    def features(h, c):
+        return pl.ds(pl.multiple_of((h * 2 + c) * feat, feat), feat)
+
+    def up_first(j, _):
+        cols = pl.ds(pl.multiple_of(j * width, width), width)
+        acc = dot(rows[0, core, 0], up[features(0, core), cols], 1, 0)
+        preact[:, cols] = acc + dot(rows[0, core, 1], up[features(1, core), cols], 1, 0)
+
     def up_step(j, _):
         cols = pl.ds(pl.multiple_of(j * width, width), width)
-        acc = jnp.zeros((columns, width), F32)
-        for q in range(4):
-            acc = acc + dot(rows[q, 0], up[q * feat : (q + 1) * feat, cols], 1, 0)
+        acc = preact[:, cols]
+        for h in range(2):
+            acc = acc + dot(rows[0, 1 - core, h], up[features(h, 1 - core), cols], 1, 0)
         preact[:, cols] = acc
         t = jnp.tanh(GELU_C * (acc + GELU_A * acc * acc * acc))
         act[0, :, cols] = (0.5 * acc * (1.0 + t)).astype(BF16)
@@ -311,7 +325,7 @@
         cols = pl.ds(pl.multiple_of(j * width, width), width)
         acc = jnp.zeros((columns, width), F32)
         for q in range(4):
-            acc = acc + dot(rows[q, 1], down[cols, q * feat : (q + 1) * feat], 1, 1)
+            acc = acc + dot(rows[1, q % 2, q // 2], down[cols, q * feat : (q + 1) * feat], 1, 1)
         v = preact[:, cols]
         t = jnp.tanh(GELU_C * (v + GELU_A * v * v * v))
         slope = 0.5 * (1.0 + t) + 0.5 * v * (1.0 - t * t) * (
@@ -341,40 +355,39 @@
         quarter(a, own)
 
     def rs_pair(a):
-        drain(part_in.at[a, 0], rs_recv.at[0, a])
-        pair[a] = (part[a, across].astype(F32) + part_in[a, 0].astype(F32)).astype(BF16)
-        start(pair.at[a], pair_in.at[a], rs_send.at[2, a], rs_recv.at[2, a], cross)
+        for i, half in enumerate((1 - xh, xh)):
+            drain(part_in.at[a, i], rs_recv.at[i, a])
+
+            def paired(s, i=i, half=half):
+                r = slice(s * experts, (s + 1) * experts)
+                mine = part[a, half * 2 + core, r, :].astype(F32)
+                return mine + part_in[a, i, r, :].astype(F32)
+
+            interleave(paired, back_buf.at[a, half], False)
+        wide_start(1, a, lambda h, peer: back_buf.at[a, h, peer])
 
     def rs_finish(a):
-        drain(part_in.at[a, 1], rs_recv.at[1, a])
-        drain(pair_in.at[a], rs_recv.at[2, a])
-
-        def result(s):
-            r = slice(s * experts, (s + 1) * experts)
-            kept = part[a, own, r, :].astype(F32) + part_in[a, 1, r, :].astype(F32)
-            return kept + pair_in[a, r, :].astype(F32)
-
-        interleave(result, x_buf.at[1, a])
+        wide_wait(1, a)
+        for i in range(nyx):
+            total = r_buf[1, a, 0, i].astype(F32) + r_buf[1, a, 1, i].astype(F32)
+            w_buf[a, :, i] = total.astype(BF16)
         z_start(1, a)
 
-    yx_start(0, 0)
-    yx_wait(0, 0)
-    deinterleave(r_buf.at[0, 0], put_rows(0))
-    ag_start(0)
-    yx_start(0, 1)
-    ag_forward(0)
-    yx_wait(0, 1)
-    deinterleave(r_buf.at[0, 1], put_rows(1))
-    ag_start(1)
-    ag_wait(0)
+    z_wait(0, 0)
+    wide_start(0, 0, lambda h, peer: z_buf.at[0, 0, :, peer])
+    z_wait(0, 1)
+    wide_start(0, 1, lambda h, peer: z_buf.at[0, 1, :, peer])
+    share(0)
     loads[3].wait()
-    lax.fori_loop(0, 4, up_step, None)
+    lax.fori_loop(0, 4, up_first, None, unroll=True)
+    share_wait(0)
+    lax.fori_loop(0, 4, up_step, None, unroll=True)
     loads[4].wait()
-    ag_forward(1)
     rs_start(0)
+    share(1)
     rs_pair(0)
-    ag_wait(1)
-    lax.fori_loop(0, 4, grad_step, None)
+    share_wait(1)
+    lax.fori_loop(0, 4, grad_step, None, unroll=True)
     rs_start(1)
     rs_pair(1)
     rs_finish(0)
@@ -403,20 +416,18 @@
     def g_wait(kind):
         drain(g_full.at[kind, 0], g_recv.at[2, kind])
 
-    yx_start(1, 0)
-    yx_wait(1, 0)
-    deinterleave(r_buf.at[1, 0], put_slot(0))
+    z_wait(1, 0)
+    deinterleave(z_buf.at[1, 0], put_slot(0), True)
     for s in range(2):
         g_part[0, s] = dot(cot_ref[...], slot[0, s], 1, 1).astype(BF16)
     g_start(0)
-    yx_start(1, 1)
     g_pair(0)
     mixed = dot(comb_bf[0], slot[0, 0], 1, 0) + dot(comb_bf[1], slot[0, 1], 1, 0)
     mixed_ref[...] = mixed.astype(BF16)
     store_mixed = pltpu.make_async_copy(mixed_ref, mixed_hbm, out_sem.at[0])
     store_mixed.start()
-    yx_wait(1, 1)
-    deinterleave(r_buf.at[1, 1], put_slot(1))
+    z_wait(1, 1)
+    deinterleave(z_buf.at[1, 1], put_slot(1), True)
     for s in range(2):
         g_part[1, s] = dot(tok, slot[1, s], 1, 1).astype(BF16)
     g_start(1)
@@ -502,8 +513,8 @@
     for trip in range(2):
         for a in range(2):
             drain(z_buf.at[trip, a, pl.ds(0, nz - 1)], a2a_send.at[trip, a, 0])
-            if nyx > 1:
-                drain(r_buf.at[trip, a, pl.ds(0, nyx - 1)], a2a_send.at[trip, a, 1])
+            drain(r_buf.at[trip, a, 0], a2a_send.at[trip, a, 1])
+            drain(r_buf.at[trip, a, 1, pl.ds(0, nyx - 1)], a2a_send.at[trip, a, 1])
     if nyx > 1:
         drain(p1.at[pl.ds(0, nyx - 1)], p_send.at[0])
         drain(v1.at[pl.ds(0, nyx - 1)], p_send.at[3])
@@ -563,22 +574,22 @@
         vmem((2, seq, experts), BF16),
         vmem((2, seq, experts), BF16),
         vmem((8 * experts, lanes), F32),
+        vmem((2, nz, nyx, 4, lanes), BF16),
         vmem((2, 2, nz, nyx, 4, lanes), BF16),
-        vmem((2, 2, nz, nyx, 4, lanes), BF16),
+        vmem((2, 2, 2, nyx, nz, 4, lanes), BF16),
         vmem((2, 2, nyx, nz, 4, lanes), BF16),
+        vmem((2, nz, nyx, 4, lanes), BF16),
         dma((2, 2, 2)),
         dma((2, 2, 2)),
-        vmem((4, 2, columns, feat), BF16),
-        dma((3, 2)),
-        dma((3, 2)),
+        vmem((2, 2, 2, columns, feat), BF16),
+        dma((2,)),
+        dma((2,)),
         vmem((columns, hidden), F32),
         vmem((2, columns, hidden), BF16),
         vmem((2, 4, columns, feat), BF16),
         vmem((2, 2, columns, feat), BF16),
-        vmem((2, columns, feat), BF16),
-        vmem((2, columns, feat), BF16),
-        dma((3, 2)),
-        dma((3, 2)),
+        dma((2, 2)),
+        dma((2, 2)),
         vmem((2, 2, experts, feat), BF16),
         vmem((2, 2, seq, experts), BF16),
         vmem((2, seq, experts), BF16),

time: 102 us -> 88.4 us (0.87)
  Pallas kernels: 101 us -> 87.7 us
    pallas_call x1, Pallas kernels: 99.1 us -> 85.8 us  [layer(): pl.pallas_call(functools.partial(kernel, dims), out_shape=(jax.ShapeDtype...]
where the time goes in v4:
time: 88.4 us; the launch traced here: 88.3 us
  Pallas kernels  87.7 us (99%)
    pallas_call x1, Pallas kernels, layer(): pl.pallas_call(functools.partial(kernel, dims), out_shape=(jax.ShapeDtype...  85.8 us
    pallas_call x1, Pallas kernels, layer(): pl.pallas_call(publish, out_shape=tuple((jax.ShapeDtypeStruct(r.shape, r....  1.81 us

profile of v4, /device:TPU:2, one launch (start us, length us, event | category | flops | bytes accessed | tf_op | source)
XLA Modules:
  0.0 88.3 jit_solution(85410065327954874)
XLA Ops:
  0.6 85.8 %shard_map.76 = (bf16[196,256]{1,0:T(8,128)(2,1)}, bf16[196,256]{1,0:T(8,128)(2,1)}, f32[8,32,256]{2,1,0:T(8,128)}) custom-call(bf16[196,256]{1,0:T(8,128)(2,1)} %tok_hbm.1, bf16[256,256]{1,0:T(8,128)(2,1)} %par_hbm.1, bf16[1024,1024]{1,0:T(8,128)(2,1)} %bitcast.3, bf16[1024,1024]{1,0:T(8,128)(2,1)} %bitcast.4, bf16[196,256]{1,0:T(8,128)(2,1)} %cot_hbm.1), custom_call_target="tpu_custom_call" | custom-call | tf_op jit(solution)/shard_map/pallas_call | solution.py:616
  86.5 1.8 %shard_map.77 = (bf16[196,256]{1,0:T(8,128)(2,1)}, bf16[196,256]{1,0:T(8,128)(2,1)}, f32[8,32,256]{2,1,0:T(8,128)}) custom-call(bf16[196,256]{1,0:T(8,128)(2,1)} %get-tuple-element.9.refs_0_, bf16[196,256]{1,0:T(8,128)(2,1)} %get-tuple-element.10.refs_1_, f32[8,32,256]{2,1,0:T(8,128)} %get-tuple-element.11.refs_2_), custom_call_target="tpu_custom_call" | custom-call | tf_op jit(solution)/shard_map/pallas_call | solution.py:630

commit v5 on v4

v5 whole, which is shorter than its diff:
```python
import functools

import jax
import jax.numpy as jnp
from jax import lax
from jax.experimental import pallas as pl
from jax.experimental.pallas import tpu as pltpu
from jax.sharding import PartitionSpec as P

SEQ = 196
BF16 = jnp.bfloat16
F32 = jnp.float32
EXPERT = ("y", "x_lo", "z")
HALF = ("x_hi", "core")
MESH = pl.DeviceIdType.MESH
GELU_C = 0.7978845608
GELU_A = 0.044715


def dot(a, b, ca, cb):
    return lax.dot_general(a, b, (((ca,), (cb,)), ((), ())), preferred_element_type=F32)


def remote(src, dst, send, recv, device):
    return pltpu.make_async_remote_copy(
        src_ref=src,
        dst_ref=dst,
        send_sem=send,
        recv_sem=recv,
        device_id=device,
        device_id_type=MESH,
    )


def drain(ref, sem):
    pltpu.make_async_copy(ref, ref, sem).wait()


def kernel(
    dims,
    tok_hbm,
    par_hbm,
    up_hbm,
    down_hbm,
    cot_hbm,
    mixed_hbm,
    gtok_hbm,
    gpar_hbm,
    tok,
    par_ref,
    cot,
    up,
    down,
    in_sem,
    out_refs,
    out_in,
    mixed_ref,
    gtok_ref,
    gpar_ref,
    out_sem,
    out_send,
    out_recv,
    par_loc,
    par,
    in_send,
    in_recv,
    lg_s1,
    lg_r2,
    lg_full,
    lg_send,
    lg_recv,
    disp,
    comb,
    disp_bf,
    comb_bf,
    stage,
    x_buf,
    z_buf,
    r_buf,
    back_buf,
    w_buf,
    a2a_send,
    a2a_recv,
    rows,
    rows_send,
    rows_recv,
    preact,
    act,
    part,
    part_in,
    rs_send,
    rs_recv,
    slot,
    g_s1,
    g_r2,
    g_send,
    g_recv,
    row_sum,
    row_in,
    p0,
    p1,
    q0,
    u1,
    v0,
    v1,
    p_send,
    p_recv,
    know_x,
    know_y,
    know_z,
):
    ny, nx, nz, zl = dims
    zh = nz // zl
    nyx = ny * nx
    experts = nyx * nz
    seq, feat = tok.shape[1:]
    lanes = feat // 2
    y, x, z = lax.axis_index("y"), lax.axis_index("x_lo"), lax.axis_index("z")
    xh, core = lax.axis_index("x_hi"), lax.axis_index("core")
    yx = y * nx + x
    own = xh * 2 + core
    across = (1 - xh) * 2 + core
    partner = {"core": 1 - core}
    cross = {"x_hi": 1 - xh}
    sent = []

    def start(src, dst, send, recv, device):
        copy = remote(src, dst, send, recv, device)
        copy.start()
        sent.append(copy)
        return copy

    moves = [(dy, dx) for dy in range(ny) for dx in range(nx) if dy + dx]
    moves.sort(key=lambda m: -min(m[0], ny - m[0]) - min(m[1], nx - m[1]))

    def yx_each(action):
        for dy, dx in moves:
            py, px = lax.rem(y + dy, ny), lax.rem(x + dx, nx)
            action(py * nx + px, {"y": py, "x_lo": px})

    def z_peer(step):
        swing = step // 2
        ahead = nz // 2 + jnp.where(lax.rem(step, 2) == 0, -swing, swing)
        peer = lax.rem(z + ahead, nz)
        return peer, {"z": peer}

    loads = []
    for i, (src, dst) in enumerate(
        (
            (tok_hbm, tok.at[core]),
            (par_hbm, par_ref),
            (cot_hbm, cot.at[core]),
            (up_hbm, up),
            (down_hbm, down),
        )
    ):
        loads.append(pltpu.make_async_copy(src, dst, in_sem.at[i]))
        loads[i].start()
    barrier = pltpu.get_barrier_semaphore()

    def greet(device):
        pl.semaphore_signal(barrier, inc=1, device_id=device, device_id_type=MESH)

    def z_near(step):
        return [{"z": lax.rem(z + step, nz)}, {"z": lax.rem(z + nz - step, nz)}]

    y_near = [{"y": lax.rem(y + 1, ny)}, {"y": lax.rem(y + ny - 1, ny)}]
    x_near = {"x_lo": lax.rem(x + 1, nx)}
    x_ring = [x_near, cross, {"x_lo": 1 - x, "x_hi": 1 - xh}]
    near = [partner] + x_ring + y_near + z_near(1) + z_near(2)
    for device in near:
        greet(device)

    def tell(sem, devices):
        for device in devices:
            pl.semaphore_signal(sem, inc=1, device_id=device, device_id_type=MESH)

    columns = 2 * experts
    row_id = lax.broadcasted_iota(jnp.int32, (columns, experts), 0)
    col_id = lax.broadcasted_iota(jnp.int32, (columns, experts), 1)
    pick = [jnp.where(row_id == 2 * col_id + s, 1.0, 0.0).astype(BF16) for s in range(2)]
    loads[1].wait()
    for s in range(2):
        par_loc[s] = dot(par_ref[...], pick[s], 1, 0).astype(BF16)
    par[core] = par_loc[core]
    loads[0].wait()
    lg_s1[...] = dot(tok[core], par[core], 1, 0)

    pl.semaphore_wait(barrier, len(near))
    tell(know_z.at[0], z_near(2))
    tell(know_y, y_near)

    tok_mine, cot_mine = tok.at[core], cot.at[core]
    start(par_loc.at[1 - core], par.at[core], in_send.at[1], in_recv.at[1], partner)
    start(tok_mine, tok_mine, in_send.at[0], in_recv.at[0], partner)
    drain(par.at[0], in_recv.at[1])
    drain(tok.at[0], in_recv.at[0])
    lg_s1[...] = lg_s1[...] + dot(tok[1 - core], par[1 - core], 1, 0)
    summed_over = start(lg_s1, lg_r2, lg_send.at[0], lg_recv.at[0], cross)
    pl.semaphore_wait(know_z.at[0], 2)
    tell(know_z.at[1], z_near(4))
    pl.semaphore_wait(know_y, 2)
    tell(know_x, x_ring)
    loads[2].wait()
    start(cot_mine, cot_mine, in_send.at[2], in_recv.at[2], partner)
    summed_over.wait_recv()
    lg_full[core] = lg_s1[...] + lg_r2[...]
    mine = lg_full.at[core]
    start(mine, mine, lg_send.at[1], lg_recv.at[1], partner)

    def interleave(get, out, by_z):
        for s in range(2):
            value = get(s)
            for k in range(2):
                stage[pl.ds(s * 2 + k, experts, stride=8), :] = value[
                    :, k * lanes : (k + 1) * lanes
                ]
        for i in range(nyx):
            block = stage[i * nz * 8 : (i + 1) * nz * 8, :].reshape(nz, 8, lanes)
            if by_z:
                out[:, i] = block[:, :4, :].astype(BF16)
            else:
                out[i] = block[:, :4, :].astype(BF16)

    def deinterleave(source, put, by_z):
        fill = jnp.zeros((nz, 4, lanes), F32)
        for i in range(nyx):
            block = source[:, i] if by_z else source[i]
            block = jnp.concatenate([block.astype(F32), fill], axis=1)
            stage[i * nz * 8 : (i + 1) * nz * 8, :] = block.reshape(nz * 8, lanes)
        for s in range(2):
            for k in range(2):
                piece = stage[pl.ds(s * 2 + k, experts, stride=8), :]
                put(s, k, piece.astype(BF16))

    def z_start(trip, a):
        src, mid = (x_buf if trip == 0 else w_buf).at[a], z_buf.at[trip, a]
        s0, r0 = a2a_send.at[trip, a, 0], a2a_recv.at[trip, a, 0]

        def z_send(step, _):
            peer, device = z_peer(step)
            remote(src.at[peer], mid.at[z], s0, r0, device).start()

        lax.fori_loop(1, nz, z_send, None)
        pltpu.make_async_copy(src.at[z], mid.at[z], r0).start()

    def z_wait(trip, a):
        drain(z_buf.at[trip, a], a2a_recv.at[trip, a, 0])

    flips = [(dy, fx, fh) for dy in range(ny) for fx in range(nx) for fh in range(2)][1:]
    flips.sort(key=lambda m: -min(m[0], ny - m[0]) - (m[1] if m[1] else 2 * m[2]))

    def wide_start(trip, a, source):
        dst = r_buf.at[trip, a, xh, yx]
        s1, r1 = a2a_send.at[trip, a, 1], a2a_recv.at[trip, a, 1]
        for dy, fx, fh in flips:
            py, px = lax.rem(y + dy, ny), (1 - x if fx else x)
            ph = 1 - xh if fh else xh
            device = {"y": py, "x_lo": px, "x_hi": ph}
            remote(source(ph, py * nx + px), dst, s1, r1, device).start()
        pltpu.make_async_copy(source(xh, yx), dst, r1).start()

    def wide_wait(trip, a):
        drain(r_buf.at[trip, a], a2a_recv.at[trip, a, 1])

    w = jnp.exp(lg_full[core] - jnp.max(lg_full[core], axis=0, keepdims=True))
    w = w / jnp.sum(w, axis=0, keepdims=True)
    disp[...] = w
    disp_bf[...] = w.astype(BF16)
    interleave(lambda i: dot(disp_bf[...], tok[i], 0, 0), x_buf.at[0], True)
    pl.semaphore_wait(know_x, 3)
    pl.semaphore_wait(know_z.at[1], 2)
    z_start(0, 0)
    drain(lg_full.at[0], lg_recv.at[1])
    top = jnp.maximum(
        jnp.max(lg_full[0], axis=1, keepdims=True), jnp.max(lg_full[1], axis=1, keepdims=True)
    )
    total = jnp.sum(jnp.exp(lg_full[0] - top), axis=1, keepdims=True)
    total = total + jnp.sum(jnp.exp(lg_full[1] - top), axis=1, keepdims=True)
    w = jnp.exp(lg_full[core] - top) / total
    comb[...] = w
    comb_bf[...] = w.astype(BF16)
    drain(cot.at[0], in_recv.at[2])
    interleave(lambda i: dot(comb_bf[...], cot[i], 0, 0), x_buf.at[1], True)
    z_start(0, 1)

    def put_rows(a, h):
        def put(i, k, piece):
            rows[a, core, h, i, :, k * lanes : (k + 1) * lanes] = piece

        return put

    def share(a):
        wide_wait(0, a)
        for h in range(2):
            deinterleave(r_buf.at[0, a, h], put_rows(a, h), False)
        mine = rows.at[a, core]
        start(mine, mine, rows_send.at[a], rows_recv.at[a], partner)

    def share_wait(a):
        drain(rows.at[a, 0], rows_recv.at[a])

    hidden = up.shape[1]
    width = hidden // 4

    def up_slot(s):
        def step(j, _):
            cols = pl.ds(pl.multiple_of(j * width, width), width)
            acc = jnp.zeros((experts, width), F32)
            for q in range(4):
                acc = acc + dot(rows[0, s, q // 2, q % 2], up[q * feat : (q + 1) * feat, cols], 1, 0)
            preact[s, :, cols] = acc
            t = jnp.tanh(GELU_C * (acc + GELU_A * acc * acc * acc))
            act[0, s, :, cols] = (0.5 * acc * (1.0 + t)).astype(BF16)

        lax.fori_loop(0, 4, step, None, unroll=True)

    def grad_step(j, _):
        cols = pl.ds(pl.multiple_of(j * width, width), width)
        acc = jnp.zeros((columns, width), F32)
        for q in range(4):
            both = rows[1, :, q // 2, q % 2].reshape(columns, feat)
            acc = acc + dot(both, down[cols, q * feat : (q + 1) * feat], 1, 1)
        v = preact[:, :, cols].reshape(columns, width)
        t = jnp.tanh(GELU_C * (v + GELU_A * v * v * v))
        slope = 0.5 * (1.0 + t) + 0.5 * v * (1.0 - t * t) * (
            GELU_C * (1.0 + 3.0 * GELU_A * v * v)
        )
        act[1, :, :, cols] = (acc * slope).astype(BF16).reshape(2, experts, width)

    def quarter(a, j):
        cols = slice(j * feat, (j + 1) * feat)
        rows_in = act[a].reshape(columns, hidden)
        if a == 0:
            value = dot(rows_in, down[:, cols], 1, 0)
        else:
            value = dot(rows_in, up[cols, :], 1, 1)
        part[a, :, j] = value.astype(BF16).reshape(2, experts, feat)

    def rs_start(a):
        for h in range(2):
            quarter(a, h * 2)
            quarter(a, h * 2 + 1)
            start(
                part.at[a, 1 - core, pl.ds(h * 2, 2)],
                part_in.at[a, pl.ds(h * 2, 2)],
                rs_send.at[a, h],
                rs_recv.at[a, h],
                partner,
            )

    def rs_pair(a):
        for h in range(2):
            drain(part_in.at[a, pl.ds(h * 2, 2)], rs_recv.at[a, h])

            def paired(i, h=h):
                q = h * 2 + i
                return part[a, core, q].astype(F32) + part_in[a, q].astype(F32)

            interleave(paired, back_buf.at[a, h], False)
        wide_start(1, a, lambda h, peer: back_buf.at[a, h, peer])

    def rs_finish(a):
        wide_wait(1, a)
        for i in range(nyx):
            total = r_buf[1, a, 0, i].astype(F32) + r_buf[1, a, 1, i].astype(F32)
            w_buf[a, :, i] = total.astype(BF16)
        z_start(1, a)

    z_wait(0, 0)
    wide_start(0, 0, lambda h, peer: z_buf.at[0, 0, :, peer])
    z_wait(0, 1)
    wide_start(0, 1, lambda h, peer: z_buf.at[0, 1, :, peer])
    share(0)
    loads[3].wait()
    up_slot(core)
    share_wait(0)
    up_slot(1 - core)
    loads[4].wait()
    rs_start(0)
    share(1)
    rs_pair(0)
    share_wait(1)
    lax.fori_loop(0, 4, grad_step, None, unroll=True)
    rs_start(1)
    rs_pair(1)
    rs_finish(0)
    rs_finish(1)

    def put_slot(a):
        def put(i, k, piece):
            slot[a, i, :, k * lanes : (k + 1) * lanes] = piece

        return put

    def g_start(kind, left):
        value = dot(left[0], slot[kind, 0], 1, 1) + dot(left[1], slot[kind, 1], 1, 1)
        g_s1[kind] = value.astype(BF16)
        start(g_s1.at[kind], g_r2.at[kind], g_send.at[kind], g_recv.at[kind], cross)

    def g_get(kind):
        drain(g_r2.at[kind], g_recv.at[kind])
        return g_s1[kind].astype(F32) + g_r2[kind].astype(F32)

    def swap(kind):
        start(
            out_refs.at[kind, 1 - core],
            out_in.at[kind],
            out_send.at[kind],
            out_recv.at[kind],
            partner,
        )

    def swapped(kind):
        drain(out_in.at[kind], out_recv.at[kind])
        return (out_refs[kind, core] + out_in[kind]).astype(BF16)

    z_wait(1, 0)
    deinterleave(z_buf.at[1, 0], put_slot(0), True)
    g_start(0, cot)
    for i in range(2):
        out_refs[0, i] = dot(comb_bf[...], slot[0, i], 1, 0)
    swap(0)
    grad_comb = g_get(0)
    own_sum = jnp.sum(comb[...] * grad_comb, axis=1, keepdims=True)
    row_sum[...] = jnp.broadcast_to(own_sum, row_sum.shape)
    start(row_sum, row_in, in_send.at[3], in_recv.at[3], partner)
    z_wait(1, 1)
    deinterleave(z_buf.at[1, 1], put_slot(1), True)
    g_start(1, tok)
    drain(row_in, in_recv.at[3])
    comb[...] = comb[...] * (grad_comb - (own_sum + row_in[:, :1]))
    for i in range(2):
        out_refs[1, i] = dot(disp_bf[...], slot[1, i], 1, 0)
    mixed_ref[...] = swapped(0)
    store_mixed = pltpu.make_async_copy(mixed_ref, mixed_hbm, out_sem.at[0])
    store_mixed.start()
    gd = g_get(1)

    through = disp[...] * (gd - jnp.sum(disp[...] * gd, axis=0, keepdims=True))
    gl = (comb[...] + through).astype(BF16)

    count = nyx * zl
    piece = feat // count
    for i in range(2):
        p0[:, i] = dot(tok[i], gl, 0, 0).reshape(count, piece, experts).astype(BF16)

    low, high = lax.rem(z, zl), z // zl
    near_moves = [(dy, dx, dz) for dy in range(ny) for dx in range(nx) for dz in range(zl)][1:]
    near_moves.sort(key=lambda m: -min(m[0], ny - m[0]) - m[1] - (2 if m[2] == 2 else m[2] % 2))
    for dy, dx, dz in near_moves:
        py, px, pz = lax.rem(y + dy, ny), lax.rem(x + dx, nx), lax.rem(low + dz, zl)
        remote(
            p0.at[(py * nx + px) * zl + pz],
            p1.at[yx * zl + low],
            p_send.at[0],
            p_recv.at[0],
            {"y": py, "x_lo": px, "z": high * zl + pz},
        ).start()
    pltpu.make_async_copy(p0.at[yx * zl + low], p1.at[yx * zl + low], p_recv.at[0]).start()
    for i in range(2):
        out_refs[1, i] = out_refs[1, i] + dot(gl, par[i], 1, 1)
    swap(1)
    drain(p1, p_recv.at[0])

    value = p1[0].astype(F32)
    for i in range(1, count):
        value = value + p1[i].astype(F32)
    q0[...] = value.astype(BF16)

    def spread(step, _):
        _, device = z_peer(step)
        remote(q0, u1.at[z], p_send.at[1], p_recv.at[1], device).start()

    lax.fori_loop(1, nz, spread, None)
    pltpu.make_async_copy(q0, u1.at[z], p_recv.at[1]).start()
    gtok_ref[...] = swapped(1)
    store_gtok = pltpu.make_async_copy(gtok_ref, gtok_hbm, out_sem.at[1])
    store_gtok.start()
    drain(u1, p_recv.at[1])
    for i in range(zl):
        value = u1[i].astype(F32)
        for j in range(1, zh):
            value = value + u1[j * zl + i].astype(F32)
        v0[:, i] = value.astype(BF16)
    for dy, dx, dc in [(dy, dx, dc) for dy, dx in [*moves, (0, 0)] for dc in range(2)][:-2] + [
        (0, 0, 1)
    ]:
        py, px, pc = lax.rem(y + dy, ny), lax.rem(x + dx, nx), (1 - core if dc else core)
        remote(
            v0.at[pc],
            v1.at[core, yx],
            p_send.at[2],
            p_recv.at[2],
            {"y": py, "x_lo": px, "core": pc},
        ).start()
    pltpu.make_async_copy(v0.at[core], v1.at[core, yx], p_recv.at[2]).start()
    drain(v1, p_recv.at[2])
    value = jnp.zeros((feat, columns), F32)
    for s in range(2):
        half = v1[s].astype(F32).reshape(feat, experts).astype(BF16)
        value = value + dot(half, pick[s], 1, 1)
    gpar_ref[...] = value
    store_gpar = pltpu.make_async_copy(gpar_ref, gpar_hbm, out_sem.at[2])
    store_gpar.start()

    for copy in sent:
        copy.wait_send()
    for trip in range(2):
        for a in range(2):
            drain(z_buf.at[trip, a, pl.ds(0, nz - 1)], a2a_send.at[trip, a, 0])
            drain(r_buf.at[trip, a, 0], a2a_send.at[trip, a, 1])
            drain(r_buf.at[trip, a, 1, pl.ds(0, nyx - 1)], a2a_send.at[trip, a, 1])
    drain(p1.at[pl.ds(0, count - 1)], p_send.at[0])
    drain(u1.at[pl.ds(0, nz - 1)], p_send.at[1])
    drain(v1.at[0], p_send.at[2])
    drain(v1.at[1, pl.ds(0, nyx - 1)], p_send.at[2])
    store_mixed.wait()
    store_gtok.wait()
    store_gpar.wait()


def publish(*refs):
    sources, targets, held, sem = refs[:3], refs[3:6], refs[6:9], refs[9]
    fetch = [pltpu.make_async_copy(sources[i], held[i], sem.at[0, i]) for i in range(3)]
    store = [pltpu.make_async_copy(held[i], targets[i], sem.at[1, i]) for i in range(3)]
    for copy in fetch:
        copy.start()
    for i in range(3):
        fetch[i].wait()
        store[i].start()
    for copy in store:
        copy.wait()


def layer(dims, tokens, slot_params, w_up, w_down, cotangent):
    ny, nx, nz, zl = dims
    nyx, zh = ny * nx, nz // zl
    experts = nyx * nz
    seq, feat = tokens.shape
    columns = slot_params.shape[1]
    depth, hidden = w_up.shape[1:]
    lanes = feat // 2
    vmem, dma = pltpu.VMEM, pltpu.SemaphoreType.DMA
    piece = feat // (nyx * zl)
    scratch = [
        vmem((2, seq, feat), BF16),
        vmem((feat, columns), BF16),
        vmem((2, seq, feat), BF16),
        vmem((depth, hidden), BF16),
        vmem((hidden, depth), BF16),
        dma((5,)),
        vmem((2, 2, seq, feat), F32),
        vmem((2, seq, feat), F32),
        vmem((seq, feat), BF16),
        vmem((seq, feat), BF16),
        vmem((feat, columns), F32),
        dma((3,)),
        dma((2,)),
        dma((2,)),
        vmem((2, feat, experts), BF16),
        vmem((2, feat, experts), BF16),
        dma((4,)),
        dma((4,)),
        vmem((seq, experts), F32),
        vmem((seq, experts), F32),
        vmem((2, seq, experts), F32),
        dma((2,)),
        dma((2,)),
        vmem((seq, experts), F32),
        vmem((seq, experts), F32),
        vmem((seq, experts), BF16),
        vmem((seq, experts), BF16),
        vmem((8 * experts, lanes), F32),
        vmem((2, nz, nyx, 4, lanes), BF16),
        vmem((2, 2, nz, nyx, 4, lanes), BF16),
        vmem((2, 2, 2, nyx, nz, 4, lanes), BF16),
        vmem((2, 2, nyx, nz, 4, lanes), BF16),
        vmem((2, nz, nyx, 4, lanes), BF16),
        dma((2, 2, 2)),
        dma((2, 2, 2)),
        vmem((2, 2, 2, 2, experts, feat), BF16),
        dma((2,)),
        dma((2,)),
        vmem((2, experts, hidden), F32),
        vmem((2, 2, experts, hidden), BF16),
        vmem((2, 2, 4, experts, feat), BF16),
        vmem((2, 4, experts, feat), BF16),
        dma((2, 2)),
        dma((2, 2)),
        vmem((2, 2, experts, feat), BF16),
        vmem((2, seq, experts), BF16),
        vmem((2, seq, experts), BF16),
        dma((2,)),
        dma((2,)),
        vmem((seq, experts), F32),
        vmem((seq, experts), F32),
        vmem((nyx * zl, 2, piece, experts), BF16),
        vmem((nyx * zl, 2, piece, experts), BF16),
        vmem((2, piece, experts), BF16),
        vmem((nz, 2, piece, experts), BF16),
        vmem((2, zl, piece, experts), BF16),
        vmem((2, nyx, zl, piece, experts), BF16),
        dma((3,)),
        dma((3,)),
        pltpu.SemaphoreType.REGULAR,
        pltpu.SemaphoreType.REGULAR,
        pltpu.SemaphoreType.REGULAR((2,)),
    ]
    hbm = pl.BlockSpec(memory_space=pltpu.HBM)
    results = pl.pallas_call(
        functools.partial(kernel, dims),
        out_shape=(
            jax.ShapeDtypeStruct((seq, feat), BF16),
            jax.ShapeDtypeStruct((seq, feat), BF16),
            jax.ShapeDtypeStruct((feat, columns), F32),
        ),
        in_specs=[hbm] * 5,
        out_specs=(hbm, hbm, hbm),
        scratch_shapes=scratch,
        compiler_params=pltpu.CompilerParams(
            collective_id=0, has_side_effects=True, vmem_limit_bytes=67043328
        ),
    )(tokens, slot_params, w_up[0], w_down[0], cotangent)
    mixed, grad_tokens, grad_params = pl.pallas_call(
        publish,
        out_shape=tuple(jax.ShapeDtypeStruct(r.shape, r.dtype) for r in results),
        in_specs=[hbm] * 3,
        out_specs=(hbm, hbm, hbm),
        scratch_shapes=[vmem(r.shape, r.dtype) for r in results] + [dma((2, 3))],
        compiler_params=pltpu.CompilerParams(vmem_limit_bytes=67043328),
    )(*results)
    return mixed, grad_tokens, grad_params


def build(mesh, dims):
    in_specs = (
        P(EXPERT, HALF),
        P(HALF, None),
        P(EXPERT, None, HALF),
        P(EXPERT, HALF, None),
        P(EXPERT, HALF),
    )
    out_specs = (P(EXPERT, HALF), P(EXPERT, HALF), P(HALF, None))
    return jax.shard_map(
        functools.partial(layer, dims),
        mesh=mesh,
        in_specs=in_specs,
        out_specs=out_specs,
        check_vma=False,
    )


def solution(mesh):
    return build(
        jax.sharding.Mesh(mesh.devices.reshape(4, 2, 16, 2, 2), EXPERT + HALF), (4, 2, 16, 4)
    )
```

time: 88.4 us -> 86 us (0.973)
  the two profiles are of different devices: /device:TPU:2 before, /device:TPU:1 now
where the time goes in v5:
time: 86 us; the launch traced here: 85.9 us
  Pallas kernels  85.3 us (99%)
    pallas_call x1, Pallas kernels, layer(): pl.pallas_call(functools.partial(kernel, dims), out_shape=(jax.ShapeDtype...  83.4 us
    pallas_call x1, Pallas kernels, layer(): pl.pallas_call(publish, out_shape=tuple((jax.ShapeDtypeStruct(r.shape, r....  1.81 us

profile of v5, /device:TPU:1, one launch (start us, length us, event | category | flops | bytes accessed | tf_op | source)
XLA Modules:
  0.0 85.9 jit_solution(4407744849324986494)
XLA Ops:
  0.6 83.4 %shard_map.76 = (bf16[196,256]{1,0:T(8,128)(2,1)}, bf16[196,256]{1,0:T(8,128)(2,1)}, f32[256,256]{1,0:T(8,128)}) custom-call(bf16[196,256]{1,0:T(8,128)(2,1)} %tok_hbm.1, bf16[256,256]{1,0:T(8,128)(2,1)} %par_hbm.1, bf16[1024,1024]{1,0:T(8,128)(2,1)} %bitcast.2, bf16[1024,1024]{1,0:T(8,128)(2,1)} %bitcast.3, bf16[196,256]{1,0:T(8,128)(2,1)} %cot_hbm.1), custom_call_target="tpu_custom_call" | custom-call | tf_op jit(solution)/shard_map/pallas_call | solution.py:611
  84.1 1.8 %shard_map.77 = (bf16[196,256]{1,0:T(8,128)(2,1)}, bf16[196,256]{1,0:T(8,128)(2,1)}, f32[256,256]{1,0:T(8,128)}) custom-call(bf16[196,256]{1,0:T(8,128)(2,1)} %get-tuple-element.6.refs_0_, bf16[196,256]{1,0:T(8,128)(2,1)} %get-tuple-element.7.refs_1_, f32[256,256]{1,0:T(8,128)} %get-tuple-element.8.refs_2_), custom_call_target="tpu_custom_call" | custom-call | tf_op jit(solution)/shard_map/pallas_call | solution.py:625

commit v6 on v5

--- a/solution.py
+++ b/solution.py
@@ -250,15 +250,18 @@
     flips = [(dy, fx, fh) for dy in range(ny) for fx in range(nx) for fh in range(2)][1:]
     flips.sort(key=lambda m: -min(m[0], ny - m[0]) - (m[1] if m[1] else 2 * m[2]))
 
-    def wide_start(trip, a, source):
+    def wide_start(trip, a, source, only=None):
         dst = r_buf.at[trip, a, xh, yx]
         s1, r1 = a2a_send.at[trip, a, 1], a2a_recv.at[trip, a, 1]
         for dy, fx, fh in flips:
+            if only not in (None, fh):
+                continue
             py, px = lax.rem(y + dy, ny), (1 - x if fx else x)
             ph = 1 - xh if fh else xh
             device = {"y": py, "x_lo": px, "x_hi": ph}
             remote(source(ph, py * nx + px), dst, s1, r1, device).start()
-        pltpu.make_async_copy(source(xh, yx), dst, r1).start()
+        if only != 1:
+            pltpu.make_async_copy(source(xh, yx), dst, r1).start()
 
     def wide_wait(trip, a):
         drain(r_buf.at[trip, a], a2a_recv.at[trip, a, 1])
@@ -329,7 +332,7 @@
         act[1, :, :, cols] = (acc * slope).astype(BF16).reshape(2, experts, width)
 
     def quarter(a, j):
-        cols = slice(j * feat, (j + 1) * feat)
+        cols = pl.ds(pl.multiple_of(j * feat, feat), feat)
         rows_in = act[a].reshape(columns, hidden)
         if a == 0:
             value = dot(rows_in, down[:, cols], 1, 0)
@@ -338,7 +341,7 @@
         part[a, :, j] = value.astype(BF16).reshape(2, experts, feat)
 
     def rs_start(a):
-        for h in range(2):
+        for h in (1 - xh, xh):
             quarter(a, h * 2)
             quarter(a, h * 2 + 1)
             start(
@@ -350,7 +353,7 @@
             )
 
     def rs_pair(a):
-        for h in range(2):
+        for fh, h in ((1, 1 - xh), (0, xh)):
             drain(part_in.at[a, pl.ds(h * 2, 2)], rs_recv.at[a, h])
 
             def paired(i, h=h):
@@ -358,7 +361,7 @@
                 return part[a, core, q].astype(F32) + part_in[a, q].astype(F32)
 
             interleave(paired, back_buf.at[a, h], False)
-        wide_start(1, a, lambda h, peer: back_buf.at[a, h, peer])
+            wide_start(1, a, lambda h, peer: back_buf.at[a, h, peer], fh)
 
     def rs_finish(a):
         wide_wait(1, a)

time: 86 us -> 86.7 us (level)
  no operation moved by 1% of the time
where the time goes in v6:
time: 86.7 us; the launch traced here: 86.5 us
  Pallas kernels  85.9 us (99%)
    pallas_call x1, Pallas kernels, layer(): pl.pallas_call(functools.partial(kernel, dims), out_shape=(jax.ShapeDtype...  84.1 us
    pallas_call x1, Pallas kernels, layer(): pl.pallas_call(publish, out_shape=tuple((jax.ShapeDtypeStruct(r.shape, r....  1.81 us

profile of v6, /device:TPU:1, one launch (start us, length us, event | category | flops | bytes accessed | tf_op | source)
XLA Modules:
  0.0 86.5 jit_solution(4432968505845596421)
XLA Ops:
  0.6 84.1 %shard_map.76 = (bf16[196,256]{1,0:T(8,128)(2,1)}, bf16[196,256]{1,0:T(8,128)(2,1)}, f32[256,256]{1,0:T(8,128)}) custom-call(bf16[196,256]{1,0:T(8,128)(2,1)} %tok_hbm.1, bf16[256,256]{1,0:T(8,128)(2,1)} %par_hbm.1, bf16[1024,1024]{1,0:T(8,128)(2,1)} %bitcast.2, bf16[1024,1024]{1,0:T(8,128)(2,1)} %bitcast.3, bf16[196,256]{1,0:T(8,128)(2,1)} %cot_hbm.1), custom_call_target="tpu_custom_call" | custom-call | tf_op jit(solution)/shard_map/pallas_call | solution.py:614
  84.7 1.8 %shard_map.77 = (bf16[196,256]{1,0:T(8,128)(2,1)}, bf16[196,256]{1,0:T(8,128)(2,1)}, f32[256,256]{1,0:T(8,128)}) custom-call(bf16[196,256]{1,0:T(8,128)(2,1)} %get-tuple-element.6.refs_0_, bf16[196,256]{1,0:T(8,128)(2,1)} %get-tuple-element.7.refs_1_, f32[256,256]{1,0:T(8,128)} %get-tuple-element.8.refs_2_), custom_call_target="tpu_custom_call" | custom-call | tf_op jit(solution)/shard_map/pallas_call | solution.py:628
